TPU v7x, 32 devices: a whole 2x2x4 slice. The times are simulated.
32 devices in a mesh: row: 4 (over z), col: 8 (over y, x, core).
Axes of the slice: x: 2, y: 2, z: 4, core: 2. Of those that a mesh axis runs over, the one named last changes fastest.
Arguments:
- embedding: float32 [4096, 256], P(('row', 'col')), may hold values from -6 to 6
- seed_cluster: int32 [4096], P(('row', 'col')), may hold values from 0 to 127
Outputs:
- log_member: float32 [4096, 128], P(('row', 'col'))
All inputs are finite; a program needn't handle non-finite values.
Results may differ from a plain program's by a relative error of at most 0.0003.
Values sent between devices are 32-bit elements; how exact they have to be, the bound alone decides.
A program may use at most 64 MiB of HBM per device.

v0:
```python
import functools

import jax
import jax.numpy as jnp
from jax import lax
from jax.experimental import pallas as pl
from jax.experimental.pallas import tpu as pltpu
from jax.sharding import PartitionSpec as P

CLUSTER_COUNT = 128
SWEEPS = 2
ANNEAL_TEMP_VALUE = 0.02
MESH = pl.DeviceIdType.MESH


def flip(index, offset, size):
    out, bit = 0, 1
    while bit < size:
        out = out + bit * ((index // bit + offset // bit) % 2)
        bit *= 2
    return out


def split3(x):
    first = x.astype(jnp.bfloat16)
    rest = x - first.astype(jnp.float32)
    second = rest.astype(jnp.bfloat16)
    third = (rest - second.astype(jnp.float32)).astype(jnp.bfloat16)
    return first, second, third


def nt(a, b):
    return lax.dot_general(
        a, b, (((1,), (1,)), ((), ())), preferred_element_type=jnp.float32
    )


def nn(a, b):
    return jnp.dot(a, b, preferred_element_type=jnp.float32)


def seeds_to_member(seeds):
    points = seeds.shape[1]
    labels = lax.broadcasted_iota(jnp.int32, (CLUSTER_COUNT, points), 0)
    chosen = jnp.where(labels == seeds, 0.5, 0.0).astype(jnp.float32)
    return chosen.T + 0.5 / CLUSTER_COUNT


def kernel(
    R, C, e_ref, s_ref, o_ref,
    e_row, e_col, s_row, s_col, c1, c2, c3, csq, d1, d2, d3, m1, m2, m3, m_row,
    m_own, m_col, pp, pin, psum, rin, az_own, az_in, acc,
    er_s, er_r, rel_s, rel_r, ec_s, ec_r, sr_s, sr_r, sc_s, sc_r,
    px_s, px_r, rs_s, rs_r, az_s, az_r,
    mz_s, mz_r, mc_s, mc_r, mrel_s, mrel_r,
):
    n = e_ref.shape[0]
    Q = C // 2
    r = lax.axis_index("row")
    c = lax.axis_index("col")
    q, b = c // 2, c % 2
    started = []

    def send(src, dst, ssem, rsem, row, col):
        copy = pltpu.make_async_remote_copy(
            src_ref=src, dst_ref=dst, send_sem=ssem, recv_sem=rsem,
            device_id=(row, col), device_id_type=MESH,
        )
        copy.start()
        started.append(copy)
        return copy

    def row_peer(t):
        return flip(r, t, R)

    def chip_peer(s):
        return flip(q, s, Q)

    def col_of(chip, core):
        return chip * 2 + core

    def block(i):
        return pl.ds(i * n, n) if isinstance(i, int) else pl.ds(pl.multiple_of(i * n, n), n)

    def row_slot(s, core):
        return block(2 * s + core)

    def pair_slot(s):
        return pl.ds(2 * s * n, 2 * n)

    partner = col_of(q, 1 - b)
    group = 2 if R % 2 == 0 else 1
    groups = [list(range(g, g + group)) for g in range(0, R, group)]
    row_order = [t for t in range(2, R)] + [t for t in range(1, min(R, 2))]
    chip_order = list(range(Q - 1, 0, -1))

    def bits(size):
        return [1 << i for i in range(size.bit_length() - 1)]

    barrier = pltpu.get_barrier_semaphore()
    for t in bits(R):
        pl.semaphore_signal(barrier, inc=1, device_id=(row_peer(t), c), device_id_type=MESH)
    for u in bits(C):
        pl.semaphore_signal(barrier, inc=1, device_id=(r, flip(c, u, C)), device_id_type=MESH)

    def ready_column(x, t):
        at = block(t)
        p1, p2, p3 = split3(x)
        c1[at, :] = p1
        c2[at, :] = p2
        c3[at, :] = p3
        q1, q2, q3 = split3(x * x)
        ones = jnp.ones((8, x.shape[1]), jnp.bfloat16)
        csq[:, at] = (nt(ones, q3) + nt(ones, q2)) + nt(ones, q1)

    e_row[row_slot(0, b), :] = e_ref[...]
    own_member = seeds_to_member(s_ref[...])
    m_row[row_slot(0, b), :] = own_member
    m1[block(0), :] = own_member.astype(jnp.bfloat16)
    ready_column(e_ref[...], 0)

    pl.semaphore_wait(barrier, len(bits(R)) + len(bits(C)))

    seeds_col, seeds_rw, direct, alongz = {}, {}, {}, {}

    def send_seeds_col(u):
        seeds_col[u] = send(
            s_ref, s_row.at[(u // 2) * 2 + b], sr_s.at[u], sr_r.at[u], r, flip(c, u, C)
        )

    def send_seeds_rw(t):
        seeds_rw[t] = send(s_ref, s_col.at[t], sc_s.at[t], sc_r.at[t], row_peer(t), c)

    def send_alongz(t):
        alongz[t] = send(e_ref, e_col.at[block(t)], ec_s.at[t], ec_r.at[t], row_peer(t), c)

    def send_direct(s):
        direct[s] = send(
            e_ref, e_row.at[row_slot(s, b)], er_s.at[s], er_r.at[s], r,
            partner if s == 0 else col_of(chip_peer(s), b),
        )

    for t in bits(R):
        send_seeds_rw(t)
    for u in bits(C):
        send_seeds_col(u)
    far_rows, far_chips = bits(R)[::-1], bits(C)[:0:-1]
    for i in range(max(len(far_rows), len(far_chips))):
        if i < len(far_rows):
            send_alongz(far_rows[i])
        if i < len(far_chips):
            send_direct(far_chips[i] // 2)
    send_direct(0)

    heard_row, heard_col = set(), set()
    for t in range(1, R):
        if t not in bits(R):
            via = t - (1 << (t.bit_length() - 1))
            if via not in heard_row:
                seeds_rw[via].wait_recv()
                heard_row.add(via)
            send_seeds_rw(t)
            send_alongz(t)
    for u in range(1, C):
        if u not in bits(C):
            via = u - (1 << (u.bit_length() - 1))
            if via not in heard_col:
                seeds_col[via].wait_recv()
                heard_col.add(via)
            send_seeds_col(u)
            if u % 2 == 0:
                send_direct(u // 2)

    for u in range(1, C):
        if u not in heard_col:
            seeds_col[u].wait_recv()
        core = (b + u) % 2
        m_row[row_slot(u // 2, core), :] = seeds_to_member(s_row[(u // 2) * 2 + core])
    for t in range(1, R):
        if t not in heard_row:
            seeds_rw[t].wait_recv()
        m1[block(t), :] = seeds_to_member(s_col[t]).astype(jnp.bfloat16)

    relay = {}
    for s in range(1, Q):
        direct[s].wait_recv()
        at = row_slot(s, b)
        relay[s] = send(e_row.at[at], e_row.at[at], rel_s.at[s], rel_r.at[s], r, partner)

    def span(ts):
        return pl.ds(ts[0] * n, len(ts) * n)

    def make_distance(s, ts):
        pair, cols = pair_slot(s), span(ts)
        x = e_row[pair, :]
        x1, x2, x3 = split3(x)
        k1, k2, k3 = c1[cols, :], c2[cols, :], c3[cols, :]
        inner = nt(x3, k1) + nt(x2, k2) + nt(x1, k3)
        inner = inner + (nt(x2, k1) + nt(x1, k2))
        inner = inner + nt(x1, k1)
        sq = jnp.sum(x * x, axis=1, keepdims=True)
        distance = jnp.sqrt(sq + csq[0:1, cols] - 2.0 * inner + 1.0)
        p1, p2, p3 = split3(distance)
        d1[pair, cols] = p1
        d2[pair, cols] = p2
        d3[pair, cols] = p3
        a1 = m1[cols, :]
        return (nn(p3, a1) + nn(p2, a1)) + nn(p1, a1)

    def take_distance(s, ts):
        pair, cols = pair_slot(s), span(ts)
        p1, p2, p3 = d1[pair, cols], d2[pair, cols], d3[pair, cols]
        a1, a2, a3 = m1[cols, :], m2[cols, :], m3[cols, :]
        low = nn(p3, a1) + nn(p2, a2) + nn(p1, a3)
        return low + (nn(p2, a1) + nn(p1, a2)) + nn(p1, a1)

    log_member = None
    mz, mc, mrel = {}, {}, {}
    for w in range(SWEEPS):
        order = list(range(Q - 1, -1, -1))
        exchange, scatter = {}, {}

        def combine(s):
            exchange[s].wait_recv()
            psum[w, s] = pp[w, s, b] + pin[w, s]
            if s:
                scatter[s] = send(
                    psum.at[w, s], rin.at[w, s], rs_s.at[w, s], rs_r.at[w, s],
                    r, col_of(chip_peer(s), b),
                )

        cohesion = jnp.zeros((1, CLUSTER_COUNT), jnp.float32)
        products = make_distance if w == 0 else take_distance
        last = None
        for at, ts in enumerate(groups):
            for t in sorted(ts, reverse=True):
                if t == 0:
                    continue
                if w == 0:
                    alongz[t].wait_recv()
                    ready_column(e_col[block(t), :], t)
                else:
                    mz[t].wait_recv()
                    ready_member(m_col[block(t), :], t)
            final = at + 1 == len(groups)
            for s in (range(Q) if at == 0 else order):
                if at == 0 and w == 0:
                    (direct[0] if s == 0 else relay[s]).wait_recv()
                part = products(s, ts)
                if at:
                    part = part + acc[s]
                if not final:
                    acc[s] = part
                    continue
                pp[w, s, 0] = part[:n]
                pp[w, s, 1] = part[n:]
                exchange[s] = send(
                    pp.at[w, s, 1 - b], pin.at[w, s], px_s.at[w, s], px_r.at[w, s], r, partner
                )
                if w:
                    (mc[0] if s == 0 else mrel[s]).wait_recv()
                cohesion = cohesion + jnp.sum(
                    m_row[pair_slot(s), :] * part, axis=0, keepdims=True
                )
                if last is not None:
                    combine(last)
                last = s
            if w and at == 0:
                for s in range(1, Q):
                    mc[s].wait_recv()
                    slot = row_slot(s, b)
                    mrel[s] = send(m_row.at[slot], m_row.at[slot], mrel_s.at[s], mrel_r.at[s], r, partner)

        counts = jnp.sum(own_member, axis=0, keepdims=True)
        az_own[w, 0:1, :] = counts
        az_own[w, 1:2, :] = cohesion
        shares = {}
        for t in range(R - 1, -1, -1):
            for u in range(C - 1, -1, -1):
                if t or u:
                    i = t * C + u
                    shares[i] = send(
                        az_own.at[w], az_in.at[w, i], az_s.at[w, i], az_r.at[w, i],
                        row_peer(t), flip(c, u, C),
                    )
        combine(last)
        attraction = psum[w, 0]
        for s in order:
            if s:
                scatter[s].wait_recv()
                attraction = attraction + rin[w, s]
        for i in shares:
            shares[i].wait_recv()
        az_in[w, 0] = az_own[w]
        sums = jnp.sum(az_in[w], axis=0)
        counts, cohesion = sums[0:1, :], sums[1:2, :]
        pair_energy = attraction / counts - cohesion / (2.0 * counts * counts)
        logits = -pair_energy / ANNEAL_TEMP_VALUE
        highest = jnp.max(logits, axis=1, keepdims=True)
        total = jnp.sum(jnp.exp(logits - highest), axis=1, keepdims=True)
        log_member = logits - highest - jnp.log(total)
        if w + 1 < SWEEPS:
            own_member = jnp.exp(log_member)
            m_own[...] = own_member
            for i in range(max(R, Q) - 1):
                if i < R - 1:
                    t = row_order[i]
                    mz[t] = send(m_own, m_col.at[block(t)], mz_s.at[t], mz_r.at[t], row_peer(t), c)
                if i < Q - 1:
                    s = chip_order[i]
                    mc[s] = send(
                        m_own, m_row.at[row_slot(s, b)], mc_s.at[s], mc_r.at[s],
                        r, col_of(chip_peer(s), b),
                    )
            mc[0] = send(m_own, m_row.at[row_slot(0, b)], mc_s.at[0], mc_r.at[0], r, partner)
            m_row[row_slot(0, b), :] = own_member

            def ready_member(x, t):
                at = block(t)
                p1, p2, p3 = split3(x)
                m1[at, :] = p1
                m2[at, :] = p2
                m3[at, :] = p3

            ready_member(own_member, 0)

    o_ref[...] = log_member
    for copy in started:
        copy.wait_send()


def shards(R, C, embedding, seed_cluster):
    n, features = embedding.shape
    k = CLUSTER_COUNT
    Q = C // 2
    f32, bf16, i32 = jnp.float32, jnp.bfloat16, jnp.int32
    dma = pltpu.SemaphoreType.DMA
    V = pltpu.VMEM
    return pl.pallas_call(
        functools.partial(kernel, R, C),
        out_shape=jax.ShapeDtypeStruct((n, k), f32),
        in_specs=[pl.BlockSpec(memory_space=pltpu.VMEM)] * 2,
        out_specs=pl.BlockSpec(memory_space=pltpu.VMEM),
        scratch_shapes=[
            V((C * n, features), f32), V((R * n, features), f32),
            V((C, 1, n), i32), V((R, 1, n), i32),
            V((R * n, features), bf16), V((R * n, features), bf16), V((R * n, features), bf16),
            V((8, R * n), f32),
            V((C * n, R * n), bf16), V((C * n, R * n), bf16), V((C * n, R * n), bf16),
            V((R * n, k), bf16), V((R * n, k), bf16), V((R * n, k), bf16),
            V((C * n, k), f32),
            V((n, k), f32), V((R * n, k), f32),
            V((SWEEPS, Q, 2, n, k), f32), V((SWEEPS, Q, n, k), f32),
            V((SWEEPS, Q, n, k), f32), V((SWEEPS, Q, n, k), f32),
            V((SWEEPS, 2, k), f32), V((SWEEPS, R * C, 2, k), f32),
            V((Q, 2 * n, k), f32),
            dma((Q,)), dma((Q,)), dma((Q,)), dma((Q,)), dma((R,)), dma((R,)),
            dma((C,)), dma((C,)), dma((R,)), dma((R,)),
            dma((SWEEPS, Q)), dma((SWEEPS, Q)), dma((SWEEPS, Q)), dma((SWEEPS, Q)),
            dma((SWEEPS, R * C)), dma((SWEEPS, R * C)),
            dma((R,)), dma((R,)), dma((Q,)), dma((Q,)), dma((Q,)), dma((Q,)),
        ],
        compiler_params=pltpu.CompilerParams(
            collective_id=0, has_side_effects=True, vmem_limit_bytes=60 * 1024 * 1024
        ),
    )(embedding, seed_cluster.reshape(1, n))


def solution(mesh):
    return jax.shard_map(
        functools.partial(shards, mesh.shape["row"], mesh.shape["col"]),
        mesh=mesh,
        in_specs=(P(("row", "col"), None), P(("row", "col"))),
        out_specs=P(("row", "col"), None),
        check_vma=False,
    )
```

profile of v0, /device:TPU:0, one launch (start us, length us, event | category | flops | bytes accessed | tf_op | source)
XLA Modules:
  0.0 46.7 jit_solution(13915489282817694062)
XLA Ops:
  0.0 45.2 %shard_map.28 = f32[128,128]{1,0:T(8,128)} custom-call(f32[128,256]{1,0:T(8,128)} %e_ref.1, s32[1,128]{1,0:T(1,128)} %bitcast.1), custom_call_target="tpu_custom_call" | custom-call | tf_op jit(solution)/shard_map/pallas_call | solution.py:339
  45.2 1.5 %copy.4 = f32[128,128]{1,0:T(8,128)} copy(f32[128,128]{1,0:T(8,128)} %shard_map.28) | data formatting | bytes 131072
where the time goes:
time: 46.9 us; the launch traced here: 46.7 us
  Pallas kernels  45.2 us (96%)
  local copies, waits for them, and re-layouts  1.47 us (3%)
    pallas_call x1, Pallas kernels, shards(): pl.pallas_call(functools.partial(kernel, R, C), out_shape=jax.ShapeDtypeS...  45.2 us
    unnamed x1, local copies, waits for them, and re-layouts  1.47 us

commit v1 on v0

v1 whole, which is shorter than its diff:
```python
import functools

import jax
import jax.numpy as jnp
from jax import lax
from jax.experimental import pallas as pl
from jax.experimental.pallas import tpu as pltpu
from jax.sharding import PartitionSpec as P

CLUSTER_COUNT = 128
SWEEPS = 2
ANNEAL_TEMP_VALUE = 0.02
MESH = pl.DeviceIdType.MESH
F32, BF16, I32 = jnp.float32, jnp.bfloat16, jnp.int32


def plane_order(R):
    return [2, 0, 3, 1] if R == 4 else list(range(R))


def flip(index, offset, size):
    out, bit = 0, 1
    while bit < size:
        out = out + bit * ((index // bit + offset // bit) % 2)
        bit *= 2
    return out


def look_up(index, values):
    out = jnp.int32(values[0])
    for i, value in enumerate(values):
        if i:
            out = jnp.where(index == i, jnp.int32(value), out)
    return out


def split2(x):
    first = x.astype(BF16)
    return first, (x - first.astype(F32)).astype(BF16)


def nt(a, b):
    return lax.dot_general(a, b, (((1,), (1,)), ((), ())), preferred_element_type=F32)


def tn(a, b):
    return lax.dot_general(a, b, (((0,), (0,)), ((), ())), preferred_element_type=F32)


def nn(a, b):
    return jnp.dot(a, b, preferred_element_type=F32)


def seeds_to_member(seeds):
    points = seeds.shape[1]
    labels = lax.broadcasted_iota(I32, (CLUSTER_COUNT, points), 0)
    chosen = jnp.where(labels == seeds, 0.5, 0.0).astype(F32)
    return chosen.T + 0.5 / CLUSTER_COUNT


def kernel(
    R, C, e_hbm, s_hbm, o_ref,
    e_row, s_row, e_blk, s_blk, eh, el, rsq, xt, csq, dhl, mp, mf, m32, early,
    hrow, hz, hcoh, cs, cr, pp, pin, psum, rin, a_own, a_row, a_blk, az_own, az_in,
    in_sem, ed_s, ed_r, er_s, er_r, eb_s, eb_r, sd_s, sd_r, sr_s, sr_r, sb_s, sb_r,
    cz_s, cz_r, px_s, px_r, rs_s, rs_r, az_s, az_r, ad_s, ad_r, ar_s, ar_r, ab_s, ab_r,
):
    n = e_hbm.shape[0]
    k = CLUSTER_COUNT
    Q = C // 2
    full = (R - 1) // 2
    has_half = R % 2 == 0
    half = 1 + full
    r = lax.axis_index("row")
    c = lax.axis_index("col")
    q, b = c // 2, c % 2
    order = plane_order(R)
    place = [order.index(i) for i in range(R)]
    guest_of = {f: look_up(r, [order[(place[i] + f) % R] for i in range(R)]) for f in range(1, half + 1)}
    host_of = {f: look_up(r, [order[(place[i] - f) % R] for i in range(R)]) for f in range(1, half + 1)}
    is_host = look_up(r, [int(place[i] < R // 2) for i in range(R)]) == 1
    is_guest = look_up(r, [int(place[i] < R // 2) for i in range(R)]) == 0
    fulls = list(range(1, full + 1))
    started = []

    def remote(src, dst, ssem, rsem, row, col):
        return pltpu.make_async_remote_copy(
            src_ref=src, dst_ref=dst, send_sem=ssem, recv_sem=rsem,
            device_id=(row, col), device_id_type=MESH,
        )

    def send(*args):
        copy = remote(*args)
        copy.start()
        started.append(copy)
        return copy

    def row_peer(t):
        return flip(r, t, R)

    def chip_peer(s):
        return flip(q, s, Q) * 2 + b

    partner = q * 2 + (1 - b)

    def row_slot(s, core):
        at = (2 * s + core) * n
        return pl.ds(at if isinstance(at, int) else pl.multiple_of(at, n), n)

    def pair_slot(s):
        return pl.ds(2 * s * n, 2 * n)

    barrier = pltpu.get_barrier_semaphore()
    for s in range(1, Q):
        pl.semaphore_signal(barrier, inc=1, device_id=(r, chip_peer(s)), device_id_type=MESH)
    pl.semaphore_signal(barrier, inc=1, device_id=(r, partner), device_id_type=MESH)
    for t in range(1, R):
        pl.semaphore_signal(barrier, inc=1, device_id=(row_peer(t), c), device_id_type=MESH)

    mine = row_slot(0, b)
    own_e = pltpu.make_async_copy(e_hbm, e_row.at[mine], in_sem.at[0])
    own_s = pltpu.make_async_copy(s_hbm, s_row.at[b], in_sem.at[1])
    own_e.start()
    own_s.start()
    if has_half:
        hrow[...] = jnp.zeros_like(hrow)
        hz[...] = jnp.zeros_like(hz)
        hcoh[...] = jnp.zeros_like(hcoh)

    pl.semaphore_wait(barrier, Q + R - 1)

    def spread(src_of, row_dst, blk_dst, d_s, d_r, b_s, b_r):
        direct, guests, halves = {}, {}, []
        if has_half:
            out = [
                remote(src, dst(half - 1), ss.at[half - 1], rs.at[half - 1], host_of[half], c)
                for src, dst, ss, rs in zip(src_of, blk_dst, b_s, b_r)
            ]

            @pl.when(is_guest)
            def _():
                for copy in out:
                    copy.start()

            halves = out
        for s in [0] + list(range(1, Q)):
            direct[s] = [
                send(src, dst(s), ss.at[s], rs.at[s], r, chip_peer(s) if s else partner)
                for src, dst, ss, rs in zip(src_of, row_dst, d_s, d_r)
            ]
            if s + 1 in fulls:
                f = s + 1
                guests[f] = [
                    send(src, dst(f - 1), ss.at[f - 1], rs.at[f - 1], host_of[f], c)
                    for src, dst, ss, rs in zip(src_of, blk_dst, b_s, b_r)
                ]
        for f in fulls:
            if f not in guests:
                guests[f] = [
                    send(src, dst(f - 1), ss.at[f - 1], rs.at[f - 1], host_of[f], c)
                    for src, dst, ss, rs in zip(src_of, blk_dst, b_s, b_r)
                ]
        return direct, guests, halves

    def hear(copies):
        for copy in copies:
            copy.wait_recv()

    e_direct, e_guest, e_half = spread(
        (s_hbm, e_hbm),
        (lambda s: s_row.at[2 * s + b], lambda s: e_row.at[row_slot(s, b)]),
        (lambda f: s_blk.at[f], lambda f: e_blk.at[f]),
        (sd_s, ed_s), (sd_r, ed_r), (sb_s, eb_s), (sb_r, eb_r),
    )

    def e_relay(s):
        hear(e_direct[s])
        at = row_slot(s, b)
        return [
            send(s_row.at[2 * s + b], s_row.at[2 * s + b], sr_s.at[s], sr_r.at[s], r, partner),
            send(e_row.at[at], e_row.at[at], er_s.at[s], er_r.at[s], r, partner),
        ]

    def ready_block(t, x, member):
        p1, p2 = split2(-2.0 * x)
        xt[t, :n, :] = p1
        xt[t, n:, :] = p2
        q1, q2 = split2(x * x)
        ones = jnp.ones((8, x.shape[1]), BF16)
        csq[t] = nt(ones, q2) + nt(ones, q1) + 1.0
        m32[t] = member
        if t:
            m = member.astype(BF16)
            mf[t - 1, :n, :k] = m
            mf[t - 1, n:, :k] = m

    def ready_guest(t):
        ready_block(t, e_blk[t - 1], seeds_to_member(s_blk[t - 1]))

    def ready_rows(s):
        at = pair_slot(s)
        x = e_row[at, :]
        p1, p2 = split2(x)
        eh[at, :] = p1
        el[at, :] = p2
        rsq[at, :] = jnp.sum(x * x, axis=1, keepdims=True)
        for core in range(2):
            mp[row_slot(s, core), :k] = seeds_to_member(s_row[2 * s + core]).astype(BF16)

    def tile(t, s):
        at = pair_slot(s)
        both = nt(eh[at, :], xt[t])
        inner = both[:, :n] + (both[:, n:] + nt(el[at, :], xt[t, :n, :]))
        p1, p2 = split2(jnp.sqrt(rsq[at, :] + csq[t, 0:1, :] + inner))
        dhl[t, at, :n] = p1
        dhl[t, at, n:] = p2

    def rows_of(w, t, s):
        d = dhl[t, pair_slot(s), :]
        if w == 0:
            return nn(d, mf[t - 1, :, :k])
        both = nn(d, mf[t - 1])
        return both[:, :k] + both[:, k:]

    def block_of(w, t, first, last):
        at = pl.ds(2 * first * n, 2 * (last - first) * n)
        d = dhl[t, at, :]
        if w == 0:
            both = tn(d, mp[at, :k])
            return both[:n] + both[n:]
        both = tn(d, mp[at, :])
        return both[:n, :k] + (both[n:, :k] + both[:n, k:])

    last = Q - 1
    sums = {}

    class Sweep:
        def __init__(self, w):
            self.w, self.exchange, self.scatter, self.out, self.shares = w, {}, {}, {}, {}

        def rows(self, s):
            w = self.w
            part = hrow[s] if has_half else 0.0
            for f in fulls:
                part = part + rows_of(w, f, s)
            pp[w, s, 0] = part[:n]
            pp[w, s, 1] = part[n:]
            self.exchange[s] = send(pp.at[w, s, 1 - b], pin.at[w, s], px_s.at[w, s], px_r.at[w, s], r, partner)

        def combine(self, s):
            w = self.w
            self.exchange[s].wait_recv()
            psum[w, s] = pp[w, s, b] + pin[w, s]
            if s:
                self.scatter[s] = send(
                    psum.at[w, s], rin.at[w, s], rs_s.at[w, s], rs_r.at[w, s], r, chip_peer(s)
                )

        def block_copy(self, t):
            w = self.w
            return remote(cs.at[w, t - 1], cr.at[w, t - 1], cz_s.at[w, t - 1], cz_r.at[w, t - 1], guest_of[t], c)

        def block(self, t):
            w = self.w
            part = early[t] + block_of(w, t, last, Q)
            cs[w, t - 1] = part
            copy = self.block_copy(t)
            copy.start()
            return 2.0 * jnp.sum(m32[t] * part, axis=0, keepdims=True)

        def blocks(self):
            if has_half:
                @pl.when(is_host)
                def _():
                    hcoh[...] = self.block(half)
            cohesion = hcoh[...] if has_half else 0.0
            for f in fulls:
                cohesion = cohesion + self.block(f)
                self.out[f] = self.block_copy(f)
                started.append(self.out[f])
            return cohesion

        def share(self, cohesion):
            w = self.w
            own = early[0] + block_of(w, 0, last, Q)
            cohesion = cohesion + jnp.sum(m32[0] * own, axis=0, keepdims=True)
            az_own[w, 0:1, :] = jnp.sum(m32[0], axis=0, keepdims=True)
            az_own[w, 1:2, :] = cohesion
            for t in range(R - 1, -1, -1):
                for u in range(C - 1, -1, -1):
                    if t or u:
                        i = t * C + u
                        self.shares[i] = send(
                            az_own.at[w], az_in.at[w, i], az_s.at[w, i], az_r.at[w, i],
                            row_peer(t), flip(c, u, C),
                        )
            return own

        def attraction(self, own):
            w = self.w
            total = own + psum[w, 0]
            for s in range(1, Q):
                self.scatter[s].wait_recv()
                total = total + rin[w, s]
            for f in fulls:
                self.out[f].wait_recv()
                total = total + cr[w, f - 1]
            if has_half:
                @pl.when(is_guest)
                def _():
                    self.block_copy(half).wait_recv()
                    hz[...] = cr[w, half - 1]
                total = total + hz[...]
            return total

        def scales(self):
            w = self.w
            for i in self.shares:
                self.shares[i].wait_recv()
            az_in[w, 0] = az_own[w]
            both = jnp.sum(az_in[w], axis=0)
            inverse = 1.0 / both[0:1, :]
            return inverse, (both[1:2, :] * inverse) * (0.5 * inverse)

    def logits_of(attraction, scales):
        inverse, shift = scales
        logits = (attraction * inverse - shift) * (-1.0 / ANNEAL_TEMP_VALUE)
        return logits - jnp.max(logits, axis=1, keepdims=True)

    def member_of(attraction, scales):
        top = jnp.exp(logits_of(attraction, scales))
        return top * (1.0 / jnp.sum(top, axis=1, keepdims=True))

    own_e.wait()
    own_s.wait()
    ready_block(0, e_row[mine, :], seeds_to_member(s_row[b]))
    hear(e_direct[0])
    ready_rows(0)
    tile(0, 0)
    relays = {s: e_relay(s) for s in range(1, last)}
    if has_half:
        @pl.when(is_host)
        def _():
            hear(e_half)
            ready_guest(half)
            tile(half, 0)
    for s in range(1, last):
        hear(relays[s])
        ready_rows(s)
        tile(0, s)
        if has_half:
            @pl.when(is_host)
            def _():
                tile(half, s)
    early[0] = block_of(0, 0, 0, last)
    if has_half:
        @pl.when(is_host)
        def _():
            early[half] = block_of(0, half, 0, last)
            for s in range(last):
                hrow[s] = rows_of(0, half, s)
    relays[last] = e_relay(last)
    sweep = Sweep(0)
    for f in fulls:
        hear(e_guest[f])
        ready_guest(f)
    for s in range(last):
        for f in fulls:
            tile(f, s)
        sweep.rows(s)
    for f in fulls:
        early[f] = block_of(0, f, 0, last)
    hear(relays[last])
    ready_rows(last)
    for f in fulls:
        tile(f, last)
    if has_half:
        @pl.when(is_host)
        def _():
            tile(half, last)
            hrow[last] = rows_of(0, half, last)
    sweep.rows(last)
    for s in range(1, last):
        sweep.combine(s)
    cohesion = sweep.blocks()
    sweep.combine(last)
    sweep.combine(0)
    tile(0, last)
    own = sweep.share(cohesion)
    attraction = sweep.attraction(own)

    a_own[...] = attraction
    a_direct, a_guest, a_half = spread(
        (a_own,),
        (lambda s: a_row.at[row_slot(s, b)],),
        (lambda f: a_blk.at[f],),
        (ad_s,), (ad_r,), (ab_s,), (ab_r,),
    )

    def a_relay(s):
        hear(a_direct[s])
        at = row_slot(s, b)
        return [send(a_row.at[at], a_row.at[at], ar_s.at[s], ar_r.at[s], r, partner)]

    scales = sweep.scales()
    sweep = Sweep(1)

    def fill_rows(s, core, member):
        p1, p2 = split2(member)
        mp[row_slot(s, core), :k] = p1
        mp[row_slot(s, core), k:] = p2

    def fill_block(t):
        member = member_of(a_blk[t - 1], scales)
        p1, p2 = split2(member)
        m32[t] = member
        mf[t - 1, :n, :k] = p1
        mf[t - 1, :n, k:] = p2
        mf[t - 1, n:, :k] = p1
        mf[t - 1, n:, k:] = jnp.zeros_like(p1)

    own_member = member_of(attraction, scales)
    m32[0] = own_member
    fill_rows(0, b, own_member)
    hear(a_direct[0])
    fill_rows(0, 1 - b, member_of(a_row[row_slot(0, 1 - b), :], scales))
    relays = {}
    for s in range(1, last):
        relays[s] = a_relay(s)
        fill_rows(s, b, member_of(a_row[row_slot(s, b), :], scales))
    for s in range(1, last):
        hear(relays[s])
        fill_rows(s, 1 - b, member_of(a_row[row_slot(s, 1 - b), :], scales))
    if last:
        relays[last] = a_relay(last)
        fill_rows(last, b, member_of(a_row[row_slot(last, b), :], scales))
    early[0] = block_of(1, 0, 0, last)
    if has_half:
        @pl.when(is_host)
        def _():
            hear(a_half)
            fill_block(half)
            early[half] = block_of(1, half, 0, last)
            for s in range(Q):
                hrow[s] = rows_of(1, half, s)
    for f in fulls:
        hear(a_guest[f])
        fill_block(f)
    for s in list(range(1, Q)) + [0]:
        sweep.rows(s)
    for f in fulls:
        early[f] = block_of(1, f, 0, last)
    for s in range(1, Q):
        sweep.combine(s)
    hear(relays[last])
    fill_rows(last, 1 - b, member_of(a_row[row_slot(last, 1 - b), :], scales))
    cohesion = sweep.blocks()
    own = sweep.share(cohesion)
    sweep.combine(0)
    attraction = sweep.attraction(own)
    logits = logits_of(attraction, sweep.scales())
    o_ref[...] = logits - jnp.log(jnp.sum(jnp.exp(logits), axis=1, keepdims=True))

    for copy in started:
        copy.wait_send()
    if has_half:
        @pl.when(is_guest)
        def _():
            for copy in e_half + a_half:
                copy.wait_send()

        @pl.when(is_host)
        def _():
            for w in range(SWEEPS):
                Sweep(w).block_copy(half).wait_send()


def shards(R, C, embedding, seed_cluster):
    n, features = embedding.shape
    k = CLUSTER_COUNT
    Q = C // 2
    B = 1 + (R - 1) // 2 + (R % 2 == 0)
    G = max(B - 1, 1)
    dma = pltpu.SemaphoreType.DMA
    V = pltpu.VMEM
    W = SWEEPS
    return pl.pallas_call(
        functools.partial(kernel, R, C),
        out_shape=jax.ShapeDtypeStruct((n, k), F32),
        in_specs=[pl.BlockSpec(memory_space=pl.ANY)] * 2,
        out_specs=pl.BlockSpec(memory_space=pltpu.VMEM),
        scratch_shapes=[
            V((C * n, features), F32), V((C, 1, n), I32), V((G, n, features), F32), V((G, 1, n), I32),
            V((C * n, features), BF16), V((C * n, features), BF16), V((C * n, 1), F32),
            V((B, 2 * n, features), BF16), V((B, 8, n), F32), V((B, C * n, 2 * n), BF16),
            V((C * n, 2 * k), BF16), V((G, 2 * n, 2 * k), BF16), V((B, n, k), F32), V((B, n, k), F32),
            V((Q, 2 * n, k), F32), V((n, k), F32), V((1, k), F32),
            V((W, G, n, k), F32), V((W, G, n, k), F32),
            V((W, Q, 2, n, k), F32), V((W, Q, n, k), F32), V((W, Q, n, k), F32), V((W, Q, n, k), F32),
            V((n, k), F32), V((C * n, k), F32), V((G, n, k), F32),
            V((W, 2, k), F32), V((W, R * C, 2, k), F32),
            dma((2,)), dma((Q,)), dma((Q,)), dma((Q,)), dma((Q,)), dma((G,)), dma((G,)),
            dma((Q,)), dma((Q,)), dma((Q,)), dma((Q,)), dma((G,)), dma((G,)),
            dma((W, G)), dma((W, G)), dma((W, Q)), dma((W, Q)), dma((W, Q)), dma((W, Q)),
            dma((W, R * C)), dma((W, R * C)),
            dma((Q,)), dma((Q,)), dma((Q,)), dma((Q,)), dma((G,)), dma((G,)),
        ],
        compiler_params=pltpu.CompilerParams(
            collective_id=0, has_side_effects=True, vmem_limit_bytes=60 * 1024 * 1024
        ),
    )(embedding, seed_cluster.reshape(1, n))


def solution(mesh):
    return jax.shard_map(
        functools.partial(shards, mesh.shape["row"], mesh.shape["col"]),
        mesh=mesh,
        in_specs=(P(("row", "col"), None), P(("row", "col"))),
        out_specs=P(("row", "col"), None),
        check_vma=False,
    )
```

time: 46.9 us -> 41.8 us (0.89)
  Pallas kernels: 45.2 us -> 40.1 us
    pallas_call x1, Pallas kernels: 45.2 us -> 40.1 us  [shards(): pl.pallas_call(functools.partial(kernel, R, C), out_shape=jax.ShapeDtypeS...]
where the time goes in v1:
time: 41.8 us; the launch traced here: 41.6 us
  Pallas kernels  40.1 us (96%)
  local copies, waits for them, and re-layouts  1.47 us (4%)
    pallas_call x1, Pallas kernels, shards(): pl.pallas_call(functools.partial(kernel, R, C), out_shape=jax.ShapeDtypeS...  40.1 us
    unnamed x1, local copies, waits for them, and re-layouts  1.47 us

profile of v1, /device:TPU:0, one launch (start us, length us, event | category | flops | bytes accessed | tf_op | source)
XLA Modules:
  0.0 41.6 jit_solution(882089283322376959)
XLA Ops:
  0.0 40.1 %shard_map.28 = f32[128,128]{1,0:T(8,128)} custom-call(f32[128,256]{1,0:T(8,128)} %e_hbm.1, s32[1,128]{1,0:T(1,128)} %bitcast.1), custom_call_target="tpu_custom_call" | custom-call | tf_op jit(solution)/shard_map/pallas_call | solution.py:487
  40.2 1.5 %copy.4 = f32[128,128]{1,0:T(8,128)} copy(f32[128,128]{1,0:T(8,128)} %shard_map.28) | data formatting | bytes 131072

commit v2 on v1

v2 whole, which is shorter than its diff:
```python
import functools

import jax
import jax.numpy as jnp
from jax import lax
from jax.experimental import pallas as pl
from jax.experimental.pallas import tpu as pltpu
from jax.sharding import PartitionSpec as P

CLUSTER_COUNT = 128
SWEEPS = 2
ANNEAL_TEMP_VALUE = 0.02
MESH = pl.DeviceIdType.MESH
F32, BF16, I32 = jnp.float32, jnp.bfloat16, jnp.int32


def plane_order(R):
    return [2, 0, 3, 1] if R == 4 else list(range(R))


def flip(index, offset, size):
    out, bit = 0, 1
    while bit < size:
        out = out + bit * ((index // bit + offset // bit) % 2)
        bit *= 2
    return out


def look_up(index, values):
    out = jnp.int32(values[0])
    for i, value in enumerate(values):
        if i:
            out = jnp.where(index == i, jnp.int32(value), out)
    return out


def split2(x):
    first = x.astype(BF16)
    return first, (x - first.astype(F32)).astype(BF16)


def nt(a, b):
    return lax.dot_general(a, b, (((1,), (1,)), ((), ())), preferred_element_type=F32)


def tn(a, b):
    return lax.dot_general(a, b, (((0,), (0,)), ((), ())), preferred_element_type=F32)


def nn(a, b):
    return jnp.dot(a, b, preferred_element_type=F32)


def seeds_to_member(seeds):
    points = seeds.shape[1]
    labels = lax.broadcasted_iota(I32, (CLUSTER_COUNT, points), 0)
    chosen = jnp.where(labels == seeds, 0.5, 0.0).astype(F32)
    return chosen.T + 0.5 / CLUSTER_COUNT


def kernel(
    R, C, e_hbm, s_hbm, o_ref,
    e_row, s_row, e_grp, s_grp, eh, rsq, xh, xl, csq, dhl, ma, ma32, mb,
    r0, early, psum, rin, cc, ci, cs, cr, hz, a_own, a_row, a_grp, az_own, az_in,
    in_sem, ed_s, ed_r, eg_s, eg_r, el_s, el_r, sd_s, sd_r, sg_s, sg_r, sl_s, sl_r,
    cx_s, cx_r, cz_s, cz_r, rs_s, rs_r, az_s, az_r, ad_s, ad_r, ag_s, ag_r, al_s, al_r,
):
    n = e_hbm.shape[0]
    k = CLUSTER_COUNT
    Q = C // 2
    full = (R - 1) // 2
    has_half = R % 2 == 0
    half = 1 + full
    r = lax.axis_index("row")
    c = lax.axis_index("col")
    q, b = c // 2, c % 2
    order = plane_order(R)
    place = [order.index(i) for i in range(R)]
    guest_of = {f: look_up(r, [order[(place[i] + f) % R] for i in range(R)]) for f in range(1, half + 1)}
    host_of = {f: look_up(r, [order[(place[i] - f) % R] for i in range(R)]) for f in range(1, half + 1)}
    host_flag = look_up(r, [int(place[i] < R // 2) for i in range(R)])
    is_host = host_flag == 1
    is_guest = host_flag == 0
    fulls = list(range(1, full + 1))
    guests = fulls + ([half] if has_half else [])
    groups = [0] + guests
    last = Q - 1
    near = list(range(1, last))
    far = list(range(last, 0, -1))
    offsets = sorted(range(Q), key=lambda s: bin(s).count("1"))
    partner = q * 2 + (1 - b)
    started = []

    def remote(src, dst, ssem, rsem, row, col):
        return pltpu.make_async_remote_copy(
            src_ref=src, dst_ref=dst, send_sem=ssem, recv_sem=rsem,
            device_id=(row, col), device_id_type=MESH,
        )

    def start(copies):
        for copy in copies:
            copy.start()
            started.append(copy)
        return copies

    def hear(copies):
        for copy in copies:
            copy.wait_recv()

    def row_peer(t):
        return flip(r, t, R)

    def chip_peer(s):
        return flip(q, offsets[s], Q) * 2 + b

    def slot(s, count=1):
        return pl.ds(s * n, count * n)

    barrier = pltpu.get_barrier_semaphore()
    for s in range(1, Q):
        pl.semaphore_signal(barrier, inc=1, device_id=(r, chip_peer(s)), device_id_type=MESH)
    pl.semaphore_signal(barrier, inc=1, device_id=(r, partner), device_id_type=MESH)
    for t in range(1, R):
        pl.semaphore_signal(barrier, inc=1, device_id=(row_peer(t), c), device_id_type=MESH)
    own = [
        pltpu.make_async_copy(e_hbm, e_row.at[slot(0)], in_sem.at[0]),
        pltpu.make_async_copy(s_hbm, s_row.at[0], in_sem.at[1]),
        pltpu.make_async_copy(e_hbm, e_grp.at[0, b], in_sem.at[2]),
        pltpu.make_async_copy(s_hbm, s_grp.at[0, b], in_sem.at[3]),
    ]
    for copy in own:
        copy.start()
    if has_half:
        @pl.when(is_guest)
        def _():
            e_grp[half] = jnp.zeros(e_grp.shape[1:], F32)
            s_grp[half] = jnp.zeros(s_grp.shape[1:], I32)
            a_grp[half] = jnp.zeros(a_grp.shape[1:], F32)

        hz[...] = jnp.zeros_like(hz)
    pl.semaphore_wait(barrier, Q + R - 1)

    class Spread:
        def __init__(self, srcs, rows, grps, d_s, d_r, g_s, g_r, l_s, l_r, chips):
            self.grps, self.l_s, self.l_r = grps, l_s, l_r
            self.guest = {
                t: [
                    remote(src, grp.at[t, b], ss.at[t - 1], rs.at[t - 1], host_of[t], c)
                    for src, grp, ss, rs in zip(srcs, grps, g_s, g_r)
                ]
                for t in guests
            }
            self.direct = {
                s: [
                    remote(
                        src, row(s) if s else grp.at[0, b], ss.at[s], rs.at[s],
                        r, chip_peer(s) if s else partner,
                    )
                    for src, row, grp, ss, rs in zip(srcs, rows, grps, d_s, d_r)
                ]
                for s in range(Q)
            }
            for f in fulls:
                start(self.guest[f])
            start(self.direct[0])
            if has_half:
                @pl.when(is_guest)
                def _():
                    for copy in self.guest[half]:
                        copy.start()

            for s in chips:
                start(self.direct[s])

        def relay(self, t):
            return [
                remote(grp.at[t, b], grp.at[t, b], ss.at[t - 1], rs.at[t - 1], r, partner)
                for grp, ss, rs in zip(self.grps, self.l_s, self.l_r)
            ]

        def pass_on(self, t):
            hear(self.guest[t])
            for copy in self.relay(t):
                copy.start()

        def pass_half(self):
            if has_half:
                @pl.when(is_host)
                def _():
                    self.pass_on(half)

        def hear_half(self):
            if has_half:
                @pl.when(is_host)
                def _():
                    hear(self.relay(half))

        def finish(self):
            for f in fulls:
                for copy in self.relay(f):
                    copy.wait_send()
            if has_half:
                @pl.when(is_guest)
                def _():
                    for copy in self.guest[half]:
                        copy.wait_send()

                @pl.when(is_host)
                def _():
                    for copy in self.relay(half):
                        copy.wait_send()

    points = Spread(
        (s_hbm, e_hbm), (lambda s: s_row.at[s], lambda s: e_row.at[slot(s)]), (s_grp, e_grp),
        (sd_s, ed_s), (sd_r, ed_r), (sg_s, eg_s), (sg_r, eg_r), (sl_s, el_s), (sl_r, el_r), range(1, Q),
    )

    def masked(t, member):
        return jnp.where(is_host, member, 0.0) if has_half and t == half else member

    def put_group(w, t, core, member):
        p1, p2 = split2(masked(t, member))
        for low in range(2):
            at = slot(4 * t + 2 * low + core)
            mb[at, :k] = p1
            if w:
                mb[at, k:] = jnp.zeros_like(p2) if low else p2

    def put_rows(w, s, member):
        p1, p2 = split2(member)
        ma32[slot(s), :] = member
        ma[slot(s), :k] = p1
        if w:
            ma[slot(s), k:] = p2

    def ready_group(t):
        x = e_grp[t].reshape(2 * n, e_hbm.shape[1])
        p1, p2 = split2(-2.0 * x)
        xh[t] = p1
        xl[t] = p2
        q1, q2 = split2(x * x)
        ones = jnp.ones((8, x.shape[1]), BF16)
        csq[t] = nt(ones, q2) + nt(ones, q1) + 1.0
        for core in range(2):
            put_group(0, t, core, seeds_to_member(s_grp[t, core]))

    def ready_rows(s):
        x = e_row[slot(s), :]
        p1, p2 = split2(x)
        eh[s, :n, :] = p1
        eh[s, n:, :] = p2
        rsq[s] = jnp.sum(x * x, axis=1, keepdims=True)
        put_rows(0, s, seeds_to_member(s_row[s]))

    def tile(t, s):
        both = nt(eh[s], xh[t])
        inner = both[:n] + (both[n:] + nt(eh[s, :n, :], xl[t]))
        p1, p2 = split2(jnp.sqrt(rsq[s] + csq[t, 0:1, :] + inner))
        dhl[slot(s), slot(4 * t, 2)] = p1
        dhl[slot(s), slot(4 * t + 2, 2)] = p2

    def rows_of(w, t0, t1, s0, s1):
        d = dhl[slot(s0, s1 - s0), slot(4 * t0, 4 * (t1 - t0))]
        m = slot(4 * t0, 4 * (t1 - t0))
        if w == 0:
            return nn(d, mb[m, :k])
        both = nn(d, mb[m, :])
        return both[:, :k] + both[:, k:]

    def group_of(w, t, s0, s1):
        d = dhl[slot(s0, s1 - s0), slot(4 * t, 4)]
        if w == 0:
            both = tn(d, ma[slot(s0, s1 - s0), :k])
            return both[: 2 * n] + both[2 * n :]
        both = tn(d, ma[slot(s0, s1 - s0), :])
        return both[: 2 * n, :k] + (both[2 * n :, :k] + both[: 2 * n, k:])

    class Sweep:
        def __init__(self, w):
            self.w, self.scatter, self.shares, self.parts = w, {}, {}, []

        def rows(self, s, own_part):
            w = self.w
            guest_part = rows_of(w, 1, len(groups), s, s + 1)
            part = own_part + guest_part
            psum[w, s] = part
            if s:
                self.scatter[s] = start([
                    remote(psum.at[w, s], rin.at[w, s], rs_s.at[w, s], rs_r.at[w, s], r, chip_peer(s))
                ])
            self.parts.append(jnp.sum(ma32[slot(s), :] * (part + guest_part), axis=0, keepdims=True))

        def cross(self, t):
            w = self.w
            return remote(cc.at[w, t - 1, 1 - b], ci.at[w, t - 1], cx_s.at[w, t - 1], cx_r.at[w, t - 1], r, partner)

        def away(self, t):
            w = self.w
            return remote(cs.at[w, t - 1], cr.at[w, t - 1], cz_s.at[w, t - 1], cz_r.at[w, t - 1], guest_of[t], c)

        def group(self, t, part):
            w = self.w
            cc[w, t - 1, 0] = part[:n]
            cc[w, t - 1, 1] = part[n:]
            start([self.cross(t)])

        def send_groups(self):
            w = self.w
            for t in guests:
                self.cross(t).wait_recv()
                cs[w, t - 1] = cc[w, t - 1, b] + ci[w, t - 1]
                if t in fulls:
                    start([self.away(t)])
                else:
                    @pl.when(is_host)
                    def _():
                        self.away(t).start()

        def share(self):
            w = self.w
            cohesion = self.parts[0]
            for part in self.parts[1:]:
                cohesion = cohesion + part
            az_own[w, 0:1, :] = jnp.sum(ma32[slot(0), :], axis=0, keepdims=True)
            az_own[w, 1:2, :] = cohesion
            for t in range(R - 1, -1, -1):
                for u in range(C - 1, -1, -1):
                    if t or u:
                        i = t * C + u
                        self.shares[i] = start([
                            remote(
                                az_own.at[w], az_in.at[w, i], az_s.at[w, i], az_r.at[w, i],
                                row_peer(t), flip(c, u, C),
                            )
                        ])

        def attraction(self):
            w = self.w
            total = psum[w, 0]
            for s in far:
                hear(self.scatter[s])
                total = total + rin[w, s]
            for f in fulls:
                self.away(f).wait_recv()
                total = total + cr[w, f - 1]
            if has_half:
                @pl.when(is_guest)
                def _():
                    self.away(half).wait_recv()
                    hz[...] = cr[w, half - 1]
                total = total + hz[...]
            return total

        def scales(self):
            w = self.w
            for i in self.shares:
                hear(self.shares[i])
            az_in[w, 0] = az_own[w]
            both = jnp.sum(az_in[w], axis=0)
            inverse = 1.0 / both[0:1, :]
            return inverse, (both[1:2, :] * inverse) * (0.5 * inverse)

        def finish(self):
            if has_half:
                @pl.when(is_host)
                def _():
                    self.away(half).wait_send()

    def logits_of(attraction, scales):
        inverse, shift = scales
        logits = (attraction * inverse - shift) * (-1.0 / ANNEAL_TEMP_VALUE)
        return logits - jnp.max(logits, axis=1, keepdims=True)

    def member_of(attraction, scales):
        top = jnp.exp(logits_of(attraction, scales))
        return top * (1.0 / jnp.sum(top, axis=1, keepdims=True))

    sweep = Sweep(0)
    for copy in own:
        copy.wait()
    ready_rows(0)
    hear(points.direct[0])
    ready_group(0)
    tile(0, 0)
    for s in near:
        hear(points.direct[s])
        ready_rows(s)
        tile(0, s)
    for f in fulls:
        points.pass_on(f)
    for f in fulls:
        hear(points.relay(f))
        ready_group(f)
    points.pass_half()
    for f in fulls:
        for s in range(last):
            tile(f, s)
    points.hear_half()
    if has_half:
        ready_group(half)
        for s in range(last):
            tile(half, s)
    for s in near + [0]:
        sweep.rows(s, rows_of(0, 0, 1, s, s + 1))
    for t in guests:
        early[t - 1] = group_of(0, t, 0, last)
    hear(points.direct[last])
    ready_rows(last)
    for t in groups:
        tile(t, last)
    for t in guests:
        sweep.group(t, early[t - 1] + group_of(0, t, last, Q))
    sweep.rows(last, rows_of(0, 0, 1, last, Q))
    sweep.send_groups()
    sweep.share()
    attraction = sweep.attraction()

    a_own[...] = attraction
    sums = Spread(
        (a_own,), (lambda s: a_row.at[slot(s)],), (a_grp,),
        (ad_s,), (ad_r,), (ag_s,), (ag_r,), (al_s,), (al_r,), far,
    )
    scales = sweep.scales()
    first, sweep = sweep, Sweep(1)
    own_member = member_of(attraction, scales)
    put_rows(1, 0, own_member)
    a_grp[0, b] = attraction
    hear(sums.direct[0])
    for core in range(2):
        put_group(1, 0, core, member_of(a_grp[0, core], scales))
    r0[...] = rows_of(1, 0, 1, 0, Q)
    for f in fulls:
        sums.pass_on(f)
    for s in far:
        hear(sums.direct[s])
        put_rows(1, s, member_of(a_row[slot(s), :], scales))
    sums.pass_half()
    for t in guests:
        sweep.group(t, group_of(1, t, 0, Q))
    for f in fulls:
        hear(sums.relay(f))
        for core in range(2):
            put_group(1, f, core, member_of(a_grp[f, core], scales))
    sums.hear_half()
    if has_half:
        for core in range(2):
            put_group(1, half, core, member_of(a_grp[half, core], scales))
    for s in far + [0]:
        sweep.rows(s, r0[slot(s), :])
    sweep.send_groups()
    sweep.share()
    attraction = sweep.attraction()
    logits = logits_of(attraction, sweep.scales())
    o_ref[...] = logits - jnp.log(jnp.sum(jnp.exp(logits), axis=1, keepdims=True))

    for copy in started:
        copy.wait_send()
    for part in (points, sums, first, sweep):
        part.finish()


def shards(R, C, embedding, seed_cluster):
    n, features = embedding.shape
    k = CLUSTER_COUNT
    Q = C // 2
    B = 1 + (R - 1) // 2 + (R % 2 == 0)
    G = max(B - 1, 1)
    dma = pltpu.SemaphoreType.DMA
    V = pltpu.VMEM
    W = SWEEPS
    return pl.pallas_call(
        functools.partial(kernel, R, C),
        out_shape=jax.ShapeDtypeStruct((n, k), F32),
        in_specs=[pl.BlockSpec(memory_space=pl.ANY)] * 2,
        out_specs=pl.BlockSpec(memory_space=pltpu.VMEM),
        scratch_shapes=[
            V((Q * n, features), F32), V((Q, 1, n), I32), V((B, 2, n, features), F32), V((B, 2, 1, n), I32),
            V((Q, 2 * n, features), BF16), V((Q, n, 1), F32),
            V((B, 2 * n, features), BF16), V((B, 2 * n, features), BF16), V((B, 8, 2 * n), F32),
            V((Q * n, B * 4 * n), BF16), V((Q * n, 2 * k), BF16), V((Q * n, k), F32), V((B * 4 * n, 2 * k), BF16),
            V((Q * n, k), F32), V((G, 2 * n, k), F32),
            V((W, Q, n, k), F32), V((W, Q, n, k), F32), V((W, G, 2, n, k), F32),
            V((W, G, n, k), F32), V((W, G, n, k), F32), V((W, G, n, k), F32), V((n, k), F32),
            V((n, k), F32), V((Q * n, k), F32), V((B, 2, n, k), F32),
            V((W, 2, k), F32), V((W, R * C, 2, k), F32),
            dma((4,)), dma((Q,)), dma((Q,)), dma((G,)), dma((G,)), dma((G,)), dma((G,)),
            dma((Q,)), dma((Q,)), dma((G,)), dma((G,)), dma((G,)), dma((G,)),
            dma((W, G)), dma((W, G)), dma((W, G)), dma((W, G)), dma((W, Q)), dma((W, Q)),
            dma((W, R * C)), dma((W, R * C)),
            dma((Q,)), dma((Q,)), dma((G,)), dma((G,)), dma((G,)), dma((G,)),
        ],
        compiler_params=pltpu.CompilerParams(
            collective_id=0, has_side_effects=True, vmem_limit_bytes=56426496
        ),
    )(embedding, seed_cluster.reshape(1, n))


def solution(mesh):
    return jax.shard_map(
        functools.partial(shards, mesh.shape["row"], mesh.shape["col"]),
        mesh=mesh,
        in_specs=(P(("row", "col"), None), P(("row", "col"))),
        out_specs=P(("row", "col"), None),
        check_vma=False,
    )
```

time: 41.8 us -> 39.6 us (0.947)
  Pallas kernels: 40.1 us -> 38.1 us
    pallas_call x1, Pallas kernels: 40.1 us -> 38.1 us  [shards(): pl.pallas_call(functools.partial(kernel, R, C), out_shape=jax.ShapeDtypeS...]
    unnamed x1 -> x3, local copies, waits for them, and re-layouts: 1.47 us -> 1.29 us
where the time goes in v2:
time: 39.6 us; the launch traced here: 39.4 us
  Pallas kernels  38.1 us (96%)
  local copies, waits for them, and re-layouts  1.29 us (3%)
    pallas_call x1, Pallas kernels, shards(): pl.pallas_call(functools.partial(kernel, R, C), out_shape=jax.ShapeDtypeS...  38.1 us
    unnamed x3, local copies, waits for them, and re-layouts  1.29 us

profile of v2, /device:TPU:0, one launch (start us, length us, event | category | flops | bytes accessed | tf_op | source)
XLA Modules:
  0.0 39.4 jit_solution(780836718678654768)
XLA Ops:
  0.0 0.0 copy-start
  0.0 0.7 %copy-done = s32[128]{0:T(128)S(1)} copy-done((s32[128]{0:T(128)S(1)}, s32[128]{0:T(128)}, u32[]{:S(2)}) %copy-start) | copy-done | bytes 536
  0.7 38.1 %shard_map.28 = f32[128,128]{1,0:T(8,128)S(1)} custom-call(f32[128,256]{1,0:T(8,128)} %e_hbm.1, s32[1,128]{1,0:T(1,128)S(1)} %bitcast.1), custom_call_target="tpu_custom_call" | custom-call | tf_op jit(solution)/shard_map/pallas_call | solution.py:471
  38.8 0.6 %copy.4 = f32[128,128]{1,0:T(8,128)} copy(f32[128,128]{1,0:T(8,128)S(1)} %shard_map.28) | data formatting | bytes 131072
Async XLA Ops:
  0.0 0.7 %copy-start = (s32[128]{0:T(128)S(1)}, s32[128]{0:T(128)}, u32[]{:S(2)}) copy-start(s32[128]{0:T(128)} %param.3) | copy-start | bytes 1540

commit v3 on v2

--- a/solution.py
+++ b/solution.py
@@ -61,7 +61,7 @@
 def kernel(
     R, C, e_hbm, s_hbm, o_ref,
     e_row, s_row, e_grp, s_grp, eh, rsq, xh, xl, csq, dhl, ma, ma32, mb,
-    r0, early, psum, rin, cc, ci, cs, cr, hz, a_own, a_row, a_grp, az_own, az_in,
+    r0, r1, early, psum, rin, cc, ci, cs, cr, hz, a_own, a_row, a_grp, az_own, az_in,
     in_sem, ed_s, ed_r, eg_s, eg_r, el_s, el_r, sd_s, sd_r, sg_s, sg_r, sl_s, sl_r,
     cx_s, cx_r, cz_s, cz_r, rs_s, rs_r, az_s, az_r, ad_s, ad_r, ag_s, ag_r, al_s, al_r,
 ):
@@ -88,7 +88,6 @@
     near = list(range(1, last))
     far = list(range(last, 0, -1))
     offsets = sorted(range(Q), key=lambda s: bin(s).count("1"))
-    partner = q * 2 + (1 - b)
     started = []
 
     def remote(src, dst, ssem, rsem, row, col):
@@ -107,11 +106,13 @@
         for copy in copies:
             copy.wait_recv()
 
-    def row_peer(t):
-        return flip(r, t, R)
+    row_peers = [flip(r, t, R) for t in range(R)]
+    col_peers = [flip(c, u, C) for u in range(C)]
+
+    partner = col_peers[1]
 
     def chip_peer(s):
-        return flip(q, offsets[s], Q) * 2 + b
+        return col_peers[2 * offsets[s]]
 
     def slot(s, count=1):
         return pl.ds(s * n, count * n)
@@ -120,32 +121,38 @@
     for s in range(1, Q):
         pl.semaphore_signal(barrier, inc=1, device_id=(r, chip_peer(s)), device_id_type=MESH)
     pl.semaphore_signal(barrier, inc=1, device_id=(r, partner), device_id_type=MESH)
-    for t in range(1, R):
-        pl.semaphore_signal(barrier, inc=1, device_id=(row_peer(t), c), device_id_type=MESH)
+    for f in fulls:
+        pl.semaphore_signal(barrier, inc=1, device_id=(guest_of[f], c), device_id_type=MESH)
+    if has_half:
+        @pl.when(is_host)
+        def _():
+            pl.semaphore_signal(barrier, inc=1, device_id=(guest_of[half], c), device_id_type=MESH)
+
     own = [
         pltpu.make_async_copy(e_hbm, e_row.at[slot(0)], in_sem.at[0]),
         pltpu.make_async_copy(s_hbm, s_row.at[0], in_sem.at[1]),
-        pltpu.make_async_copy(e_hbm, e_grp.at[0, b], in_sem.at[2]),
-        pltpu.make_async_copy(s_hbm, s_grp.at[0, b], in_sem.at[3]),
+        pltpu.make_async_copy(e_hbm, e_grp.at[0, 0], in_sem.at[2]),
+        pltpu.make_async_copy(s_hbm, s_grp.at[0, 0], in_sem.at[3]),
     ]
     for copy in own:
         copy.start()
     if has_half:
         @pl.when(is_guest)
         def _():
-            e_grp[half] = jnp.zeros(e_grp.shape[1:], F32)
-            s_grp[half] = jnp.zeros(s_grp.shape[1:], I32)
-            a_grp[half] = jnp.zeros(a_grp.shape[1:], F32)
+            for core in range(2):
+                e_grp[core, half] = jnp.zeros(e_grp.shape[2:], F32)
+                s_grp[core, half] = jnp.zeros(s_grp.shape[2:], I32)
+                a_grp[core, half] = jnp.zeros(a_grp.shape[2:], F32)
 
         hz[...] = jnp.zeros_like(hz)
-    pl.semaphore_wait(barrier, Q + R - 1)
+    pl.semaphore_wait(barrier, Q + full + (1 - host_flag if has_half else 0))
 
     class Spread:
         def __init__(self, srcs, rows, grps, d_s, d_r, g_s, g_r, l_s, l_r, chips):
             self.grps, self.l_s, self.l_r = grps, l_s, l_r
             self.guest = {
                 t: [
-                    remote(src, grp.at[t, b], ss.at[t - 1], rs.at[t - 1], host_of[t], c)
+                    remote(src, grp.at[0, t], ss.at[t - 1], rs.at[t - 1], host_of[t], c)
                     for src, grp, ss, rs in zip(srcs, grps, g_s, g_r)
                 ]
                 for t in guests
@@ -153,7 +160,7 @@
             self.direct = {
                 s: [
                     remote(
-                        src, row(s) if s else grp.at[0, b], ss.at[s], rs.at[s],
+                        src, row(s) if s else grp.at[1, 0], ss.at[s], rs.at[s],
                         r, chip_peer(s) if s else partner,
                     )
                     for src, row, grp, ss, rs in zip(srcs, rows, grps, d_s, d_r)
@@ -174,7 +181,7 @@
 
         def relay(self, t):
             return [
-                remote(grp.at[t, b], grp.at[t, b], ss.at[t - 1], rs.at[t - 1], r, partner)
+                remote(grp.at[0, t], grp.at[1, t], ss.at[t - 1], rs.at[t - 1], r, partner)
                 for grp, ss, rs in zip(self.grps, self.l_s, self.l_r)
             ]
 
@@ -215,16 +222,21 @@
         (sd_s, ed_s), (sd_r, ed_r), (sg_s, eg_s), (sg_r, eg_r), (sl_s, el_s), (sl_r, el_r), range(1, Q),
     )
 
-    def masked(t, member):
-        return jnp.where(is_host, member, 0.0) if has_half and t == half else member
-
-    def put_group(w, t, core, member):
-        p1, p2 = split2(masked(t, member))
+    B = len(groups)
+
+    def span(core, t0, t1, width=1):
+        return slot((core * B + t0) * width, (t1 - t0) * width)
+
+    def put_group(w, core, t, member):
+        if has_half and t == half:
+            member = jnp.where(is_host, member, 0.0)
+        p1, p2 = split2(member)
         for low in range(2):
-            at = slot(4 * t + 2 * low + core)
+            at = slot((core * B + t) * 2 + low)
             mb[at, :k] = p1
             if w:
                 mb[at, k:] = jnp.zeros_like(p2) if low else p2
+        return member
 
     def put_rows(w, s, member):
         p1, p2 = split2(member)
@@ -233,16 +245,16 @@
         if w:
             ma[slot(s), k:] = p2
 
-    def ready_group(t):
-        x = e_grp[t].reshape(2 * n, e_hbm.shape[1])
+    def ready_group(core, t):
+        x = e_grp[core, t]
         p1, p2 = split2(-2.0 * x)
-        xh[t] = p1
-        xl[t] = p2
+        at = span(core, t, t + 1)
+        xh[at, :] = p1
+        xl[at, :] = p2
         q1, q2 = split2(x * x)
         ones = jnp.ones((8, x.shape[1]), BF16)
-        csq[t] = nt(ones, q2) + nt(ones, q1) + 1.0
-        for core in range(2):
-            put_group(0, t, core, seeds_to_member(s_grp[t, core]))
+        csq[:, at] = nt(ones, q2) + nt(ones, q1) + 1.0
+        put_group(0, core, t, seeds_to_member(s_grp[core, t]))
 
     def ready_rows(s):
         x = e_row[slot(s), :]
@@ -252,63 +264,66 @@
         rsq[s] = jnp.sum(x * x, axis=1, keepdims=True)
         put_rows(0, s, seeds_to_member(s_row[s]))
 
-    def tile(t, s):
-        both = nt(eh[s], xh[t])
-        inner = both[:n] + (both[n:] + nt(eh[s, :n, :], xl[t]))
-        p1, p2 = split2(jnp.sqrt(rsq[s] + csq[t, 0:1, :] + inner))
-        dhl[slot(s), slot(4 * t, 2)] = p1
-        dhl[slot(s), slot(4 * t + 2, 2)] = p2
-
-    def rows_of(w, t0, t1, s0, s1):
-        d = dhl[slot(s0, s1 - s0), slot(4 * t0, 4 * (t1 - t0))]
-        m = slot(4 * t0, 4 * (t1 - t0))
+    def tile(core, t0, t1, s):
+        at = span(core, t0, t1)
+        both = nt(eh[s], xh[at, :])
+        inner = both[:n] + (both[n:] + nt(eh[s, :n, :], xl[at, :]))
+        p1, p2 = split2(jnp.sqrt(rsq[s] + csq[0:1, at] + inner))
+        for t in range(t0, t1):
+            part = slice((t - t0) * n, (t - t0 + 1) * n)
+            dhl[slot(s), slot((core * B + t) * 2)] = p1[:, part]
+            dhl[slot(s), slot((core * B + t) * 2 + 1)] = p2[:, part]
+
+    def rows_of(w, core, t0, t1, s0, s1):
+        at = span(core, t0, t1, 2)
+        d = dhl[slot(s0, s1 - s0), at]
         if w == 0:
-            return nn(d, mb[m, :k])
-        both = nn(d, mb[m, :])
+            return nn(d, mb[at, :k])
+        both = nn(d, mb[at, :])
         return both[:, :k] + both[:, k:]
 
-    def group_of(w, t, s0, s1):
-        d = dhl[slot(s0, s1 - s0), slot(4 * t, 4)]
-        if w == 0:
-            both = tn(d, ma[slot(s0, s1 - s0), :k])
-            return both[: 2 * n] + both[2 * n :]
-        both = tn(d, ma[slot(s0, s1 - s0), :])
-        return both[: 2 * n, :k] + (both[2 * n :, :k] + both[: 2 * n, k:])
+    def groups_of(w, core, s0, s1):
+        rows = slot(s0, s1 - s0)
+        both = tn(dhl[rows, span(core, 1, B, 2)], ma[rows, :k] if w == 0 else ma[rows, :])
+        if w:
+            both = both[:, :k] + both[:, k:]
+        return [both[2 * i * n : (2 * i + 1) * n] + both[(2 * i + 1) * n : (2 * i + 2) * n] for i in range(B - 1)]
+
+    def over(member, sums):
+        return jnp.sum(member * sums, axis=0, keepdims=True)
 
     class Sweep:
         def __init__(self, w):
             self.w, self.scatter, self.shares, self.parts = w, {}, {}, []
 
-        def rows(self, s, own_part):
-            w = self.w
-            guest_part = rows_of(w, 1, len(groups), s, s + 1)
-            part = own_part + guest_part
-            psum[w, s] = part
-            if s:
-                self.scatter[s] = start([
-                    remote(psum.at[w, s], rin.at[w, s], rs_s.at[w, s], rs_r.at[w, s], r, chip_peer(s))
-                ])
-            self.parts.append(jnp.sum(ma32[slot(s), :] * (part + guest_part), axis=0, keepdims=True))
+        def rows(self, s, own_part, guest_part):
+            psum[self.w, s] = own_part + guest_part
+
+        def send_rows(self, s):
+            w = self.w
+            self.scatter[s] = start([
+                remote(psum.at[w, s], rin.at[w, s], rs_s.at[w, s], rs_r.at[w, s], r, chip_peer(s))
+            ])
 
         def cross(self, t):
             w = self.w
-            return remote(cc.at[w, t - 1, 1 - b], ci.at[w, t - 1], cx_s.at[w, t - 1], cx_r.at[w, t - 1], r, partner)
+            return remote(cc.at[w, t - 1], ci.at[w, t - 1], cx_s.at[w, t - 1], cx_r.at[w, t - 1], r, partner)
 
         def away(self, t):
             w = self.w
             return remote(cs.at[w, t - 1], cr.at[w, t - 1], cz_s.at[w, t - 1], cz_r.at[w, t - 1], guest_of[t], c)
 
-        def group(self, t, part):
-            w = self.w
-            cc[w, t - 1, 0] = part[:n]
-            cc[w, t - 1, 1] = part[n:]
-            start([self.cross(t)])
-
-        def send_groups(self):
+        def cross_groups(self, parts):
+            for t in guests:
+                cc[self.w, t - 1] = parts[t - 1]
+            for t in guests:
+                start([self.cross(t)])
+
+        def send_groups(self, parts):
             w = self.w
             for t in guests:
                 self.cross(t).wait_recv()
-                cs[w, t - 1] = cc[w, t - 1, b] + ci[w, t - 1]
+                cs[w, t - 1] = parts[t - 1] + ci[w, t - 1]
                 if t in fulls:
                     start([self.away(t)])
                 else:
@@ -316,21 +331,24 @@
                     def _():
                         self.away(t).start()
 
-        def share(self):
+        def total(self):
             w = self.w
             cohesion = self.parts[0]
             for part in self.parts[1:]:
                 cohesion = cohesion + part
             az_own[w, 0:1, :] = jnp.sum(ma32[slot(0), :], axis=0, keepdims=True)
             az_own[w, 1:2, :] = cohesion
+
+        def share(self, us):
+            w = self.w
             for t in range(R - 1, -1, -1):
-                for u in range(C - 1, -1, -1):
+                for u in us:
                     if t or u:
                         i = t * C + u
                         self.shares[i] = start([
                             remote(
                                 az_own.at[w], az_in.at[w, i], az_s.at[w, i], az_r.at[w, i],
-                                row_peer(t), flip(c, u, C),
+                                row_peers[t], col_peers[u],
                             )
                         ])
 
@@ -379,40 +397,62 @@
     for copy in own:
         copy.wait()
     ready_rows(0)
+    ready_group(0, 0)
+    tile(0, 0, 1, 0)
     hear(points.direct[0])
-    ready_group(0)
-    tile(0, 0)
+    ready_group(1, 0)
+    tile(1, 0, 1, 0)
     for s in near:
         hear(points.direct[s])
         ready_rows(s)
-        tile(0, s)
+        for core in range(2):
+            tile(core, 0, 1, s)
     for f in fulls:
         points.pass_on(f)
+        ready_group(0, f)
+    for f in fulls:
+        for s in range(last):
+            tile(0, f, f + 1, s)
+    points.pass_half()
     for f in fulls:
         hear(points.relay(f))
-        ready_group(f)
-    points.pass_half()
+        ready_group(1, f)
     for f in fulls:
         for s in range(last):
-            tile(f, s)
+            tile(1, f, f + 1, s)
     points.hear_half()
     if has_half:
-        ready_group(half)
-        for s in range(last):
-            tile(half, s)
-    for s in near + [0]:
-        sweep.rows(s, rows_of(0, 0, 1, s, s + 1))
-    for t in guests:
-        early[t - 1] = group_of(0, t, 0, last)
+        for core in range(2):
+            ready_group(core, half)
+            for s in range(last):
+                tile(core, half, half + 1, s)
+    both = rows_of(0, 0, 1, B, 0, last) + rows_of(0, 1, 1, B, 0, last)
+    mine = rows_of(0, 0, 0, 1, 0, last) + rows_of(0, 1, 0, 1, 0, last)
+    for s in range(last):
+        own_part, guest_part = mine[s * n : (s + 1) * n], both[s * n : (s + 1) * n]
+        sweep.rows(s, own_part, guest_part)
+        sweep.parts.append(over(ma32[slot(s), :], own_part + 2.0 * guest_part))
+    for s in near:
+        sweep.send_rows(s)
+    for core in range(2):
+        for i, part in enumerate(groups_of(0, core, 0, last)):
+            early[core, i] = part
     hear(points.direct[last])
     ready_rows(last)
-    for t in groups:
-        tile(t, last)
-    for t in guests:
-        sweep.group(t, early[t - 1] + group_of(0, t, last, Q))
-    sweep.rows(last, rows_of(0, 0, 1, last, Q))
-    sweep.send_groups()
-    sweep.share()
+    tile(1, 1, B, last)
+    sweep.cross_groups([early[1, i] + part for i, part in enumerate(groups_of(0, 1, last, Q))])
+    tile(0, 1, B, last)
+    parts = [early[0, i] + part for i, part in enumerate(groups_of(0, 0, last, Q))]
+    for core in range(2):
+        tile(core, 0, 1, last)
+    own_part = rows_of(0, 0, 0, 1, last, Q) + rows_of(0, 1, 0, 1, last, Q)
+    guest_part = rows_of(0, 0, 1, B, last, Q) + rows_of(0, 1, 1, B, last, Q)
+    sweep.rows(last, own_part, guest_part)
+    sweep.parts.append(over(ma32[slot(last), :], own_part + 2.0 * guest_part))
+    sweep.send_rows(last)
+    sweep.send_groups(parts)
+    sweep.total()
+    sweep.share(range(C - 1, -1, -1))
     attraction = sweep.attraction()
 
     a_own[...] = attraction
@@ -424,31 +464,38 @@
     first, sweep = sweep, Sweep(1)
     own_member = member_of(attraction, scales)
     put_rows(1, 0, own_member)
-    a_grp[0, b] = attraction
+    put_group(1, 0, 0, own_member)
     hear(sums.direct[0])
-    for core in range(2):
-        put_group(1, 0, core, member_of(a_grp[0, core], scales))
-    r0[...] = rows_of(1, 0, 1, 0, Q)
+    put_group(1, 1, 0, member_of(a_grp[1, 0], scales))
+    r0[...] = rows_of(1, 0, 0, 1, 0, Q) + rows_of(1, 1, 0, 1, 0, Q)
+    sweep.parts.append(over(own_member, r0[slot(0), :]))
     for f in fulls:
         sums.pass_on(f)
     for s in far:
         hear(sums.direct[s])
-        put_rows(1, s, member_of(a_row[slot(s), :], scales))
+        member = member_of(a_row[slot(s), :], scales)
+        put_rows(1, s, member)
+        sweep.parts.append(over(member, r0[slot(s), :]))
+    cross = groups_of(1, 1, 0, Q)
+    sweep.cross_groups(cross)
     sums.pass_half()
+    parts = groups_of(1, 0, 0, Q)
     for t in guests:
-        sweep.group(t, group_of(1, t, 0, Q))
+        sweep.parts.append(over(put_group(1, 0, t, member_of(a_grp[0, t], scales)), 2.0 * parts[t - 1]))
+    r1[...] = rows_of(1, 0, 1, B, 0, Q)
     for f in fulls:
         hear(sums.relay(f))
-        for core in range(2):
-            put_group(1, f, core, member_of(a_grp[f, core], scales))
     sums.hear_half()
-    if has_half:
-        for core in range(2):
-            put_group(1, half, core, member_of(a_grp[half, core], scales))
+    for t in guests:
+        sweep.parts.append(over(put_group(1, 1, t, member_of(a_grp[1, t], scales)), 2.0 * cross[t - 1]))
+    sweep.total()
+    sweep.share(range(C - 1, -1, -1))
+    sweep.send_groups(parts)
+    both = r1[...] + rows_of(1, 1, 1, B, 0, Q)
     for s in far + [0]:
-        sweep.rows(s, r0[slot(s), :])
-    sweep.send_groups()
-    sweep.share()
+        sweep.rows(s, r0[slot(s), :], both[s * n : (s + 1) * n])
+        if s:
+            sweep.send_rows(s)
     attraction = sweep.attraction()
     logits = logits_of(attraction, sweep.scales())
     o_ref[...] = logits - jnp.log(jnp.sum(jnp.exp(logits), axis=1, keepdims=True))
@@ -474,14 +521,14 @@
         in_specs=[pl.BlockSpec(memory_space=pl.ANY)] * 2,
         out_specs=pl.BlockSpec(memory_space=pltpu.VMEM),
         scratch_shapes=[
-            V((Q * n, features), F32), V((Q, 1, n), I32), V((B, 2, n, features), F32), V((B, 2, 1, n), I32),
+            V((Q * n, features), F32), V((Q, 1, n), I32), V((2, B, n, features), F32), V((2, B, 1, n), I32),
             V((Q, 2 * n, features), BF16), V((Q, n, 1), F32),
-            V((B, 2 * n, features), BF16), V((B, 2 * n, features), BF16), V((B, 8, 2 * n), F32),
+            V((2 * B * n, features), BF16), V((2 * B * n, features), BF16), V((8, 2 * B * n), F32),
             V((Q * n, B * 4 * n), BF16), V((Q * n, 2 * k), BF16), V((Q * n, k), F32), V((B * 4 * n, 2 * k), BF16),
-            V((Q * n, k), F32), V((G, 2 * n, k), F32),
-            V((W, Q, n, k), F32), V((W, Q, n, k), F32), V((W, G, 2, n, k), F32),
+            V((Q * n, k), F32), V((Q * n, k), F32), V((2, G, n, k), F32),
+            V((W, Q, n, k), F32), V((W, Q, n, k), F32), V((W, G, n, k), F32),
             V((W, G, n, k), F32), V((W, G, n, k), F32), V((W, G, n, k), F32), V((n, k), F32),
-            V((n, k), F32), V((Q * n, k), F32), V((B, 2, n, k), F32),
+            V((n, k), F32), V((Q * n, k), F32), V((2, B, n, k), F32),
             V((W, 2, k), F32), V((W, R * C, 2, k), F32),
             dma((4,)), dma((Q,)), dma((Q,)), dma((G,)), dma((G,)), dma((G,)), dma((G,)),
             dma((Q,)), dma((Q,)), dma((G,)), dma((G,)), dma((G,)), dma((G,)),

time: 39.6 us -> 38.3 us (0.967)
  Pallas kernels: 38.1 us -> 36.9 us
    pallas_call x1, Pallas kernels: 38.1 us -> 36.9 us  [shards(): pl.pallas_call(functools.partial(kernel, R, C), out_shape=jax.ShapeDtypeS...]
where the time goes in v3:
time: 38.3 us; the launch traced here: 38.2 us
  Pallas kernels  36.9 us (96%)
  local copies, waits for them, and re-layouts  1.29 us (3%)
    pallas_call x1, Pallas kernels, shards(): pl.pallas_call(functools.partial(kernel, R, C), out_shape=jax.ShapeDtypeS...  36.9 us
    unnamed x3, local copies, waits for them, and re-layouts  1.29 us

profile of v3, /device:TPU:0, one launch (start us, length us, event | category | flops | bytes accessed | tf_op | source)
XLA Modules:
  0.0 38.2 jit_solution(16762368150042921086)
XLA Ops:
  0.0 0.0 copy-start
  0.0 0.7 %copy-done = s32[128]{0:T(128)S(1)} copy-done((s32[128]{0:T(128)S(1)}, s32[128]{0:T(128)}, u32[]{:S(2)}) %copy-start) | copy-done | bytes 536
  0.7 36.9 %shard_map.28 = f32[128,128]{1,0:T(8,128)S(1)} custom-call(f32[128,256]{1,0:T(8,128)} %e_hbm.1, s32[1,128]{1,0:T(1,128)S(1)} %bitcast.1), custom_call_target="tpu_custom_call" | custom-call | tf_op jit(solution)/shard_map/pallas_call | solution.py:518
  37.6 0.6 %copy.4 = f32[128,128]{1,0:T(8,128)} copy(f32[128,128]{1,0:T(8,128)S(1)} %shard_map.28) | data formatting | bytes 131072
Async XLA Ops:
  0.0 0.7 %copy-start = (s32[128]{0:T(128)S(1)}, s32[128]{0:T(128)}, u32[]{:S(2)}) copy-start(s32[128]{0:T(128)} %param.3) | copy-start | bytes 1540

commit v4 on v3

--- a/solution.py
+++ b/solution.py
@@ -9,6 +9,7 @@
 
 CLUSTER_COUNT = 128
 SWEEPS = 2
+PIECES = 1
 ANNEAL_TEMP_VALUE = 0.02
 MESH = pl.DeviceIdType.MESH
 F32, BF16, I32 = jnp.float32, jnp.bfloat16, jnp.int32
@@ -61,7 +62,7 @@
 def kernel(
     R, C, e_hbm, s_hbm, o_ref,
     e_row, s_row, e_grp, s_grp, eh, rsq, xh, xl, csq, dhl, ma, ma32, mb,
-    r0, r1, early, psum, rin, cc, ci, cs, cr, hz, a_own, a_row, a_grp, az_own, az_in,
+    r0, r1, psum, rin, cc, ci, cs, cr, hz, a_own, a_row, a_grp, az_own, az_in,
     in_sem, ed_s, ed_r, eg_s, eg_r, el_s, el_r, sd_s, sd_r, sg_s, sg_r, sl_s, sl_r,
     cx_s, cx_r, cz_s, cz_r, rs_s, rs_r, az_s, az_r, ad_s, ad_r, ag_s, ag_r, al_s, al_r,
 ):
@@ -86,8 +87,8 @@
     groups = [0] + guests
     last = Q - 1
     near = list(range(1, last))
-    far = list(range(last, 0, -1))
-    offsets = sorted(range(Q), key=lambda s: bin(s).count("1"))
+    far = list(range(1, Q))
+    offsets = sorted(range(Q), key=lambda s: (s > 0, -bin(s).count("1")))
     started = []
 
     def remote(src, dst, ssem, rsem, row, col):
@@ -118,9 +119,6 @@
         return pl.ds(s * n, count * n)
 
     barrier = pltpu.get_barrier_semaphore()
-    for s in range(1, Q):
-        pl.semaphore_signal(barrier, inc=1, device_id=(r, chip_peer(s)), device_id_type=MESH)
-    pl.semaphore_signal(barrier, inc=1, device_id=(r, partner), device_id_type=MESH)
     for f in fulls:
         pl.semaphore_signal(barrier, inc=1, device_id=(guest_of[f], c), device_id_type=MESH)
     if has_half:
@@ -128,6 +126,9 @@
         def _():
             pl.semaphore_signal(barrier, inc=1, device_id=(guest_of[half], c), device_id_type=MESH)
 
+    for s in far:
+        pl.semaphore_signal(barrier, inc=1, device_id=(r, chip_peer(s)), device_id_type=MESH)
+    pl.semaphore_signal(barrier, inc=1, device_id=(r, partner), device_id_type=MESH)
     own = [
         pltpu.make_async_copy(e_hbm, e_row.at[slot(0)], in_sem.at[0]),
         pltpu.make_async_copy(s_hbm, s_row.at[0], in_sem.at[1]),
@@ -262,6 +263,8 @@
         eh[s, :n, :] = p1
         eh[s, n:, :] = p2
         rsq[s] = jnp.sum(x * x, axis=1, keepdims=True)
+
+    def ready_seeds(s):
         put_rows(0, s, seeds_to_member(s_row[s]))
 
     def tile(core, t0, t1, s):
@@ -295,6 +298,8 @@
     class Sweep:
         def __init__(self, w):
             self.w, self.scatter, self.shares, self.parts = w, {}, {}, []
+            count = PIECES if w == 0 else 1
+            self.pieces = [pl.ds(h * (n // count), n // count) for h in range(count)]
 
         def rows(self, s, own_part, guest_part):
             psum[self.w, s] = own_part + guest_part
@@ -302,16 +307,21 @@
         def send_rows(self, s):
             w = self.w
             self.scatter[s] = start([
-                remote(psum.at[w, s], rin.at[w, s], rs_s.at[w, s], rs_r.at[w, s], r, chip_peer(s))
+                remote(
+                    psum.at[w, s, at], rin.at[w, s, at], rs_s.at[w, h, s], rs_r.at[w, h, s], r, chip_peer(s)
+                )
+                for h, at in enumerate(self.pieces)
             ])
 
         def cross(self, t):
             w = self.w
             return remote(cc.at[w, t - 1], ci.at[w, t - 1], cx_s.at[w, t - 1], cx_r.at[w, t - 1], r, partner)
 
-        def away(self, t):
-            w = self.w
-            return remote(cs.at[w, t - 1], cr.at[w, t - 1], cz_s.at[w, t - 1], cz_r.at[w, t - 1], guest_of[t], c)
+        def away(self, t, h):
+            w, at = self.w, self.pieces[h]
+            return remote(
+                cs.at[w, t - 1, at], cr.at[w, t - 1, at], cz_s.at[w, h, t - 1], cz_r.at[w, h, t - 1], guest_of[t], c
+            )
 
         def cross_groups(self, parts):
             for t in guests:
@@ -324,12 +334,20 @@
             for t in guests:
                 self.cross(t).wait_recv()
                 cs[w, t - 1] = parts[t - 1] + ci[w, t - 1]
-                if t in fulls:
-                    start([self.away(t)])
-                else:
-                    @pl.when(is_host)
-                    def _():
-                        self.away(t).start()
+                if t == guests[0]:
+                    self.send_away(t, 0)
+            for h in range(len(self.pieces)):
+                for t in guests:
+                    if h or t != guests[0]:
+                        self.send_away(t, h)
+
+        def send_away(self, t, h):
+            if t in fulls:
+                start([self.away(t, h)])
+            else:
+                @pl.when(is_host)
+                def _():
+                    self.away(t, h).start()
 
         def total(self):
             w = self.w
@@ -352,21 +370,21 @@
                             )
                         ])
 
-        def attraction(self):
-            w = self.w
-            total = psum[w, 0]
+        def attraction(self, h):
+            w, at = self.w, self.pieces[h]
+            total = psum[w, 0, at]
             for s in far:
-                hear(self.scatter[s])
-                total = total + rin[w, s]
+                hear(self.scatter[s][h : h + 1])
+                total = total + rin[w, s, at]
             for f in fulls:
-                self.away(f).wait_recv()
-                total = total + cr[w, f - 1]
+                self.away(f, h).wait_recv()
+                total = total + cr[w, f - 1, at]
             if has_half:
                 @pl.when(is_guest)
                 def _():
-                    self.away(half).wait_recv()
-                    hz[...] = cr[w, half - 1]
-                total = total + hz[...]
+                    self.away(half, h).wait_recv()
+                    hz[at] = cr[w, half - 1, at]
+                total = total + hz[at]
             return total
 
         def scales(self):
@@ -382,7 +400,8 @@
             if has_half:
                 @pl.when(is_host)
                 def _():
-                    self.away(half).wait_send()
+                    for h in range(len(self.pieces)):
+                        self.away(half, h).wait_send()
 
     def logits_of(attraction, scales):
         inverse, shift = scales
@@ -396,36 +415,47 @@
     sweep = Sweep(0)
     for copy in own:
         copy.wait()
+    ready_seeds(0)
     ready_rows(0)
     ready_group(0, 0)
     tile(0, 0, 1, 0)
     hear(points.direct[0])
     ready_group(1, 0)
     tile(1, 0, 1, 0)
-    for s in near:
+    def next_rows(s, ts):
         hear(points.direct[s])
+        ready_seeds(s)
         ready_rows(s)
         for core in range(2):
-            tile(core, 0, 1, s)
+            for t in ts:
+                tile(core, t, t + 1, s)
+
+    for s in near[:1]:
+        next_rows(s, [0])
     for f in fulls:
         points.pass_on(f)
         ready_group(0, f)
-    for f in fulls:
-        for s in range(last):
+        for s in [0] + near[:1]:
             tile(0, f, f + 1, s)
-    points.pass_half()
     for f in fulls:
         hear(points.relay(f))
         ready_group(1, f)
-    for f in fulls:
-        for s in range(last):
+        for s in [0] + near[:1]:
             tile(1, f, f + 1, s)
+    points.pass_half()
+    if has_half:
+        ready_group(0, half)
+        for s in [0] + near[:1]:
+            tile(0, half, half + 1, s)
+    for s in near[1:]:
+        next_rows(s, [0] + fulls)
+        if has_half:
+            tile(0, half, half + 1, s)
     points.hear_half()
     if has_half:
-        for core in range(2):
-            ready_group(core, half)
-            for s in range(last):
-                tile(core, half, half + 1, s)
+        ready_group(1, half)
+        for s in range(last):
+            tile(1, half, half + 1, s)
     both = rows_of(0, 0, 1, B, 0, last) + rows_of(0, 1, 1, B, 0, last)
     mine = rows_of(0, 0, 0, 1, 0, last) + rows_of(0, 1, 0, 1, 0, last)
     for s in range(last):
@@ -434,58 +464,66 @@
         sweep.parts.append(over(ma32[slot(s), :], own_part + 2.0 * guest_part))
     for s in near:
         sweep.send_rows(s)
-    for core in range(2):
-        for i, part in enumerate(groups_of(0, core, 0, last)):
-            early[core, i] = part
-    hear(points.direct[last])
+    hear(points.direct[last][:1])
+    ready_seeds(last)
+    hear(points.direct[last][1:])
     ready_rows(last)
     tile(1, 1, B, last)
-    sweep.cross_groups([early[1, i] + part for i, part in enumerate(groups_of(0, 1, last, Q))])
+    sweep.cross_groups(groups_of(0, 1, 0, Q))
     tile(0, 1, B, last)
-    parts = [early[0, i] + part for i, part in enumerate(groups_of(0, 0, last, Q))]
+    parts = groups_of(0, 0, 0, Q)
     for core in range(2):
         tile(core, 0, 1, last)
     own_part = rows_of(0, 0, 0, 1, last, Q) + rows_of(0, 1, 0, 1, last, Q)
     guest_part = rows_of(0, 0, 1, B, last, Q) + rows_of(0, 1, 1, B, last, Q)
     sweep.rows(last, own_part, guest_part)
     sweep.parts.append(over(ma32[slot(last), :], own_part + 2.0 * guest_part))
+    sweep.send_groups(parts)
     sweep.send_rows(last)
-    sweep.send_groups(parts)
     sweep.total()
     sweep.share(range(C - 1, -1, -1))
-    attraction = sweep.attraction()
-
-    a_own[...] = attraction
-    sums = Spread(
-        (a_own,), (lambda s: a_row.at[slot(s)],), (a_grp,),
-        (ad_s,), (ad_r,), (ag_s,), (ag_r,), (al_s,), (al_r,), far,
-    )
+
+    sums = []
+    for h, at in enumerate(sweep.pieces):
+        a_own[at] = sweep.attraction(h)
+        sums.append(Spread(
+            (a_own.at[at],),
+            (lambda s, h=h: a_row.at[pl.ds(s * n + h * (n // PIECES), n // PIECES)],),
+            (a_grp.at[:, :, at],),
+            (ad_s.at[h],), (ad_r.at[h],), (ag_s.at[h],), (ag_r.at[h],), (al_s.at[h],), (al_r.at[h],), far,
+        ))
+    attraction = a_own[...]
     scales = sweep.scales()
     first, sweep = sweep, Sweep(1)
     own_member = member_of(attraction, scales)
     put_rows(1, 0, own_member)
     put_group(1, 0, 0, own_member)
-    hear(sums.direct[0])
+    for part in sums:
+        hear(part.direct[0])
     put_group(1, 1, 0, member_of(a_grp[1, 0], scales))
     r0[...] = rows_of(1, 0, 0, 1, 0, Q) + rows_of(1, 1, 0, 1, 0, Q)
     sweep.parts.append(over(own_member, r0[slot(0), :]))
-    for f in fulls:
-        sums.pass_on(f)
+    for part in sums:
+        for f in fulls:
+            part.pass_on(f)
     for s in far:
-        hear(sums.direct[s])
+        for part in sums:
+            hear(part.direct[s])
         member = member_of(a_row[slot(s), :], scales)
         put_rows(1, s, member)
         sweep.parts.append(over(member, r0[slot(s), :]))
+    for part in sums:
+        part.pass_half()
     cross = groups_of(1, 1, 0, Q)
     sweep.cross_groups(cross)
-    sums.pass_half()
     parts = groups_of(1, 0, 0, Q)
     for t in guests:
         sweep.parts.append(over(put_group(1, 0, t, member_of(a_grp[0, t], scales)), 2.0 * parts[t - 1]))
     r1[...] = rows_of(1, 0, 1, B, 0, Q)
-    for f in fulls:
-        hear(sums.relay(f))
-    sums.hear_half()
+    for part in sums:
+        for f in fulls:
+            hear(part.relay(f))
+        part.hear_half()
     for t in guests:
         sweep.parts.append(over(put_group(1, 1, t, member_of(a_grp[1, t], scales)), 2.0 * cross[t - 1]))
     sweep.total()
@@ -496,13 +534,13 @@
         sweep.rows(s, r0[slot(s), :], both[s * n : (s + 1) * n])
         if s:
             sweep.send_rows(s)
-    attraction = sweep.attraction()
+    attraction = sweep.attraction(0)
     logits = logits_of(attraction, sweep.scales())
     o_ref[...] = logits - jnp.log(jnp.sum(jnp.exp(logits), axis=1, keepdims=True))
 
     for copy in started:
         copy.wait_send()
-    for part in (points, sums, first, sweep):
+    for part in [points, first, sweep] + sums:
         part.finish()
 
 
@@ -525,16 +563,16 @@
             V((Q, 2 * n, features), BF16), V((Q, n, 1), F32),
             V((2 * B * n, features), BF16), V((2 * B * n, features), BF16), V((8, 2 * B * n), F32),
             V((Q * n, B * 4 * n), BF16), V((Q * n, 2 * k), BF16), V((Q * n, k), F32), V((B * 4 * n, 2 * k), BF16),
-            V((Q * n, k), F32), V((Q * n, k), F32), V((2, G, n, k), F32),
+            V((Q * n, k), F32), V((Q * n, k), F32),
             V((W, Q, n, k), F32), V((W, Q, n, k), F32), V((W, G, n, k), F32),
             V((W, G, n, k), F32), V((W, G, n, k), F32), V((W, G, n, k), F32), V((n, k), F32),
             V((n, k), F32), V((Q * n, k), F32), V((2, B, n, k), F32),
             V((W, 2, k), F32), V((W, R * C, 2, k), F32),
             dma((4,)), dma((Q,)), dma((Q,)), dma((G,)), dma((G,)), dma((G,)), dma((G,)),
             dma((Q,)), dma((Q,)), dma((G,)), dma((G,)), dma((G,)), dma((G,)),
-            dma((W, G)), dma((W, G)), dma((W, G)), dma((W, G)), dma((W, Q)), dma((W, Q)),
+            dma((W, G)), dma((W, G)), dma((W, PIECES, G)), dma((W, PIECES, G)), dma((W, PIECES, Q)), dma((W, PIECES, Q)),
             dma((W, R * C)), dma((W, R * C)),
-            dma((Q,)), dma((Q,)), dma((G,)), dma((G,)), dma((G,)), dma((G,)),
+            dma((PIECES, Q)), dma((PIECES, Q)), dma((PIECES, G)), dma((PIECES, G)), dma((PIECES, G)), dma((PIECES, G)),
         ],
         compiler_params=pltpu.CompilerParams(
             collective_id=0, has_side_effects=True, vmem_limit_bytes=56426496

time: 38.3 us -> 37.9 us (0.990)
  Pallas kernels: 36.9 us -> 36.4 us
    pallas_call x1, Pallas kernels: 36.9 us -> 36.4 us  [shards(): pl.pallas_call(functools.partial(kernel, R, C), out_shape=jax.ShapeDtypeS...]
where the time goes in v4:
time: 37.9 us; the launch traced here: 37.7 us
  Pallas kernels  36.4 us (96%)
  local copies, waits for them, and re-layouts  1.29 us (3%)
    pallas_call x1, Pallas kernels, shards(): pl.pallas_call(functools.partial(kernel, R, C), out_shape=jax.ShapeDtypeS...  36.4 us
    unnamed x3, local copies, waits for them, and re-layouts  1.29 us

profile of v4, /device:TPU:0, one launch (start us, length us, event | category | flops | bytes accessed | tf_op | source)
XLA Modules:
  0.0 37.7 jit_solution(5701118532428139584)
XLA Ops:
  0.0 0.0 copy-start
  0.0 0.7 %copy-done = s32[128]{0:T(128)S(1)} copy-done((s32[128]{0:T(128)S(1)}, s32[128]{0:T(128)}, u32[]{:S(2)}) %copy-start) | copy-done | bytes 536
  0.7 36.4 %shard_map.28 = f32[128,128]{1,0:T(8,128)S(1)} custom-call(f32[128,256]{1,0:T(8,128)} %e_hbm.1, s32[1,128]{1,0:T(1,128)S(1)} %bitcast.1), custom_call_target="tpu_custom_call" | custom-call | tf_op jit(solution)/shard_map/pallas_call | solution.py:556
  37.1 0.6 %copy.4 = f32[128,128]{1,0:T(8,128)} copy(f32[128,128]{1,0:T(8,128)S(1)} %shard_map.28) | data formatting | bytes 131072
Async XLA Ops:
  0.0 0.7 %copy-start = (s32[128]{0:T(128)S(1)}, s32[128]{0:T(128)}, u32[]{:S(2)}) copy-start(s32[128]{0:T(128)} %param.3) | copy-start | bytes 1540

commit v5 on v4

--- a/solution.py
+++ b/solution.py
@@ -469,16 +469,16 @@
     hear(points.direct[last][1:])
     ready_rows(last)
     tile(1, 1, B, last)
+    tile(0, 1, B, last)
     sweep.cross_groups(groups_of(0, 1, 0, Q))
-    tile(0, 1, B, last)
-    parts = groups_of(0, 0, 0, Q)
     for core in range(2):
         tile(core, 0, 1, last)
+    parts = groups_of(0, 0, 0, Q)
+    sweep.send_groups(parts)
     own_part = rows_of(0, 0, 0, 1, last, Q) + rows_of(0, 1, 0, 1, last, Q)
     guest_part = rows_of(0, 0, 1, B, last, Q) + rows_of(0, 1, 1, B, last, Q)
     sweep.rows(last, own_part, guest_part)
     sweep.parts.append(over(ma32[slot(last), :], own_part + 2.0 * guest_part))
-    sweep.send_groups(parts)
     sweep.send_rows(last)
     sweep.total()
     sweep.share(range(C - 1, -1, -1))

time: 37.9 us -> 37.7 us (level)
  no operation moved by 1% of the time
where the time goes in v5:
time: 37.7 us; the launch traced here: 37.5 us
  Pallas kernels  36.2 us (96%)
  local copies, waits for them, and re-layouts  1.29 us (3%)
    pallas_call x1, Pallas kernels, shards(): pl.pallas_call(functools.partial(kernel, R, C), out_shape=jax.ShapeDtypeS...  36.2 us
    unnamed x3, local copies, waits for them, and re-layouts  1.29 us

profile of v5, /device:TPU:0, one launch (start us, length us, event | category | flops | bytes accessed | tf_op | source)
XLA Modules:
  0.0 37.5 jit_solution(12716143785321263023)
XLA Ops:
  0.0 0.0 copy-start
  0.0 0.7 %copy-done = s32[128]{0:T(128)S(1)} copy-done((s32[128]{0:T(128)S(1)}, s32[128]{0:T(128)}, u32[]{:S(2)}) %copy-start) | copy-done | bytes 536
  0.7 36.2 %shard_map.28 = f32[128,128]{1,0:T(8,128)S(1)} custom-call(f32[128,256]{1,0:T(8,128)} %e_hbm.1, s32[1,128]{1,0:T(1,128)S(1)} %bitcast.1), custom_call_target="tpu_custom_call" | custom-call | tf_op jit(solution)/shard_map/pallas_call | solution.py:556
  36.9 0.6 %copy.4 = f32[128,128]{1,0:T(8,128)} copy(f32[128,128]{1,0:T(8,128)S(1)} %shard_map.28) | data formatting | bytes 131072
Async XLA Ops:
  0.0 0.7 %copy-start = (s32[128]{0:T(128)S(1)}, s32[128]{0:T(128)}, u32[]{:S(2)}) copy-start(s32[128]{0:T(128)} %param.3) | copy-start | bytes 1540

commit v6 on v5

--- a/solution.py
+++ b/solution.py
@@ -493,6 +493,7 @@
             (ad_s.at[h],), (ad_r.at[h],), (ag_s.at[h],), (ag_r.at[h],), (al_s.at[h],), (al_r.at[h],), far,
         ))
     attraction = a_own[...]
+    old = len(started)
     scales = sweep.scales()
     first, sweep = sweep, Sweep(1)
     own_member = member_of(attraction, scales)
@@ -534,11 +535,13 @@
         sweep.rows(s, r0[slot(s), :], both[s * n : (s + 1) * n])
         if s:
             sweep.send_rows(s)
+    for copy in started[:old]:
+        copy.wait_send()
     attraction = sweep.attraction(0)
     logits = logits_of(attraction, sweep.scales())
     o_ref[...] = logits - jnp.log(jnp.sum(jnp.exp(logits), axis=1, keepdims=True))
 
-    for copy in started:
+    for copy in started[old:]:
         copy.wait_send()
     for part in [points, first, sweep] + sums:
         part.finish()

time: 37.7 us -> 37.6 us (level)
  no operation moved by 1% of the time
where the time goes in v6:
time: 37.6 us; the launch traced here: 37.5 us
  Pallas kernels  36.2 us (96%)
  local copies, waits for them, and re-layouts  1.29 us (3%)
    pallas_call x1, Pallas kernels, shards(): pl.pallas_call(functools.partial(kernel, R, C), out_shape=jax.ShapeDtypeS...  36.2 us
    unnamed x3, local copies, waits for them, and re-layouts  1.29 us

profile of v6, /device:TPU:0, one launch (start us, length us, event | category | flops | bytes accessed | tf_op | source)
XLA Modules:
  0.0 37.5 jit_solution(1101525270790694831)
XLA Ops:
  0.0 0.0 copy-start
  0.0 0.7 %copy-done = s32[128]{0:T(128)S(1)} copy-done((s32[128]{0:T(128)S(1)}, s32[128]{0:T(128)}, u32[]{:S(2)}) %copy-start) | copy-done | bytes 536
  0.7 36.2 %shard_map.28 = f32[128,128]{1,0:T(8,128)S(1)} custom-call(f32[128,256]{1,0:T(8,128)} %e_hbm.1, s32[1,128]{1,0:T(1,128)S(1)} %bitcast.1), custom_call_target="tpu_custom_call" | custom-call | tf_op jit(solution)/shard_map/pallas_call | solution.py:559
  36.8 0.6 %copy.4 = f32[128,128]{1,0:T(8,128)} copy(f32[128,128]{1,0:T(8,128)S(1)} %shard_map.28) | data formatting | bytes 131072
Async XLA Ops:
  0.0 0.7 %copy-start = (s32[128]{0:T(128)S(1)}, s32[128]{0:T(128)}, u32[]{:S(2)}) copy-start(s32[128]{0:T(128)} %param.3) | copy-start | bytes 1540
